TPU v7x, 32 devices: a whole 2x2x4 slice. The times are simulated.
32 devices in a mesh: dp: 4 (over z), lib: 8 (over y, x, core).
Axes of the slice: x: 2, y: 2, z: 4, core: 2. Of those that a mesh axis runs over, the one named last changes fastest.
Arguments:
- spectra: bfloat16 [12288, 512], P(('dp', 'lib')), may hold values from -6 to 6
- w_proj: bfloat16 [512, 512], replicated, may hold values from -0.25 to 0.25
- fixed_library_matrix: bfloat16 [8192, 512], P('lib')
- mol_rows: bfloat16 [65536, 512], P(('dp', 'lib'))
- cand_ids: int32 [12288, 4], P(('dp', 'lib')), may hold values from 0 to 65535, as said below
- iso_count: int32 [12288], P(('dp', 'lib')), may hold values from 1 to 3
Outputs:
- grad_w: float32 [512, 512], replicated
- grad_mol: float32 [65536, 512], P(('dp', 'lib'))
- loss: float32 [], replicated
Inputs may be any that keep to these rules, and one draw needn't show every extreme that they name: cand_ids of a spectrum on device dp, lib (in dp+lib order) name rows of the dp group's molecules: id // 2048 // 8 equals dp. Over one device's 1536 slots (all columns, live or not), at most 384 name rows whose (id // 2048) % 8 is one lib index, and exactly 384 for some lib index on every device.
All inputs are finite; a program needn't handle non-finite values.
Results may differ from a plain program's by a relative error of at most 0.0074.
Values may be sent and summed in bfloat16 or wider, within the bound.
No kernel may reach another device: no remote copies, remote signals or barrier semaphores. Data moves between devices by JAX's collectives and lax.ppermute only.
A program may use at most 64 MiB of HBM per device.

v0:
```python
import jax
import jax.numpy as jnp
from jax import lax
from jax.sharding import PartitionSpec as P

sharpness_divisor = 0.07


def absorb(state, block, spectrum_encoding):
    running_max, running_sum, derivative_tally = state
    scores = (
        lax.dot_general(
            spectrum_encoding, block, (((1,), (1,)), ((), ())), preferred_element_type=jnp.float32
        )
        / sharpness_divisor
    )
    new_max = jnp.maximum(running_max, jnp.max(scores, axis=1))
    inverse_sharpness = jnp.exp(running_max - new_max)
    weights = jnp.exp(scores - new_max[:, None])
    running_sum = running_sum * inverse_sharpness + jnp.sum(weights, axis=1)
    derivative_tally = derivative_tally * inverse_sharpness[:, None] + jnp.dot(
        weights.astype(jnp.bfloat16), block, preferred_element_type=jnp.float32
    )
    return (new_max, running_sum, derivative_tally)


def per_device(spectra, w_proj, fixed_library_matrix, mol_rows, cand_ids, iso_count):
    q_rows = spectra.shape[0]
    width = spectra.shape[1]
    mol_count = mol_rows.shape[0]
    bank_count = fixed_library_matrix.shape[0]
    lib_size = lax.axis_size("lib")
    columns = cand_ids.shape[1]
    slot_count = q_rows * columns
    capacity = 2 * slot_count // lib_size
    u_proj = jnp.dot(spectra, w_proj, preferred_element_type=jnp.float32)
    norm = jnp.sqrt(jnp.sum(u_proj * u_proj, axis=1, keepdims=True) + 1e-06)
    normalized_spectrum_matrix = u_proj / norm
    spectrum_encoding = normalized_spectrum_matrix.astype(jnp.bfloat16)
    flat_ids = cand_ids.reshape(-1)
    owner = flat_ids // mol_count % lib_size
    local_row = flat_ids % mol_count
    onehot = (owner[:, None] == jnp.arange(lib_size, dtype=jnp.int32)[None, :]).astype(jnp.int32)
    before = jnp.cumsum(onehot, axis=0) - onehot
    position = owner * capacity + jnp.sum(before * onehot, axis=1)
    requests = jnp.zeros((lib_size * capacity,), jnp.int32).at[position].set(local_row)
    requests = requests.reshape(lib_size, capacity)
    received = lax.all_to_all(requests, "lib", split_axis=0, concat_axis=0, tiled=True)
    fetched = mol_rows[received]
    returned = lax.all_to_all(fetched, "lib", split_axis=0, concat_axis=0, tiled=True)
    contender_embedding_matrix = returned.reshape(lib_size * capacity, width)[position].reshape(
        q_rows, columns, width
    )
    candidate_float_rows = contender_embedding_matrix.astype(jnp.float32)
    column = jnp.arange(columns, dtype=jnp.int32)[None, :]
    live = column <= iso_count[:, None]
    contender_similarity_values = (
        jnp.einsum(
            "ti,tmi->tm",
            spectrum_encoding,
            contender_embedding_matrix,
            preferred_element_type=jnp.float32,
        )
        / sharpness_divisor
    )
    cand_max = jnp.max(jnp.where(live, contender_similarity_values, -1e30), axis=1)
    cand_weights = jnp.where(live, jnp.exp(contender_similarity_values - cand_max[:, None]), 0.0)
    start_state = (
        cand_max,
        jnp.sum(cand_weights, axis=1),
        jnp.einsum("qk,qkd->qd", cand_weights, candidate_float_rows),
    )
    piece = lax.all_gather(fixed_library_matrix, "lib", axis=0, tiled=True)
    stacked = piece.reshape(piece.shape[0] // bank_count, bank_count, width)

    def inner(current, block):
        return (absorb(current, block, spectrum_encoding), 0)

    result, unused = lax.scan(inner, start_state, stacked)
    top, objective_aggregate, derivative_tally = result
    lse = top + jnp.log(objective_aggregate)
    scaled_cand = jnp.where(live, jnp.exp(contender_similarity_values - top[:, None]), 0.0)
    loss_terms = jnp.sum(lse - contender_similarity_values[:, 0])
    spectrum_derivative = (
        derivative_tally / objective_aggregate[:, None] - candidate_float_rows[:, 0, :]
    ) / sharpness_divisor
    grad_u = (
        (
            spectrum_derivative
            - normalized_spectrum_matrix
            * jnp.sum(normalized_spectrum_matrix * spectrum_derivative, axis=1, keepdims=True)
        )
        / norm
    ).astype(jnp.bfloat16)
    grad_local = jnp.dot(spectra.T, grad_u, preferred_element_type=jnp.float32)
    first = (column == 0).astype(jnp.float32)
    inverse_sharpness = jnp.where(live, scaled_cand / objective_aggregate[:, None] - first, 0.0)
    contender_derivative = (
        inverse_sharpness[:, :, None] * normalized_spectrum_matrix[:, None, :] / sharpness_divisor
    ).astype(jnp.bfloat16)
    outgoing = (
        jnp.zeros((lib_size * capacity, width), jnp.bfloat16)
        .at[position]
        .set(contender_derivative.reshape(slot_count, width))
    )
    incoming = lax.all_to_all(
        outgoing.reshape(lib_size, capacity, width), "lib", split_axis=0, concat_axis=0, tiled=True
    )
    grad_mol = (
        jnp.zeros((mol_count, width), jnp.float32)
        .at[received.reshape(-1)]
        .add(incoming.reshape(-1, width).astype(jnp.float32))
    )
    grad_w, loss_sum = lax.psum((grad_local, loss_terms), ("dp", "lib"))
    loss = loss_sum / (q_rows * lax.axis_size("dp") * lib_size)
    return (grad_w, grad_mol, loss)


def solution(mesh):
    placed = (
        P(("dp", "lib"), None),
        P(),
        P("lib", None),
        P(("dp", "lib"), None),
        P(("dp", "lib"), None),
        P(("dp", "lib")),
    )
    return jax.shard_map(
        per_device,
        mesh=mesh,
        in_specs=placed,
        out_specs=(P(), P(("dp", "lib"), None), P()),
        check_vma=False,
    )
```

profile of v0, /device:TPU:0, one launch (start us, length us, event | category | flops | bytes accessed | tf_op | source)
XLA Modules:
  0.0 341.9 jit_solution(17671516270576667808)
XLA Ops:
  9.2 2.3 reduce-window.6
  12.2 6.2 %scatter_custom_fusion = s32[3072]{0:T(1024)S(1)} fusion(s32[1536]{0:T(1024)S(1)} %fusion.31, s32[1536]{0:T(1024)S(1)} %get-tuple-element.64, s32[]{:T(128)} %copy.49), kind=kCustom, calls=%fused_computation.91 | custom fusion | bytes 12292 | tf_op jit(solution)/shard_map/scatter | solution.py:46
  18.4 10.0 %all_to_all.22 = s32[8,1,384]{2,1,0:T(1,128)S(1)} all-to-all(s32[8,1,384]{2,1,0:T(1,128)S(1)} %bitcast.85), channel_id=1, replica_groups=mesh['dp'=4,'lib'=8] {'lib'}, dimensions={0} | all-to-all | bytes 24576 | tf_op jit(solution)/shard_map/all_to_all | solution.py:48
  28.4 13.3 %gather_fusion = bf16[3072,512]{1,0:T(8,128)(2,1)} fusion(bf16[2048,512]{1,0:T(8,128)(2,1)S(1)} %copy-done, s32[3072]{0:T(1024)S(1)} %broadcast_clamp_fusion), kind=kCustom, calls=%fused_computation | custom fusion | bytes 6303744 | tf_op jit(solution)/shard_map/gather | solution.py:49
  41.7 4.8 %all-to-all-start.1 = ((bf16[8,384,512]{2,1,0:T(8,128)(2,1)}), bf16[8,384,512]{2,1,0:T(8,128)(2,1)}, u32[]{:S(2)}, u32[]{:S(2)}) async-start(bf16[8,384,512]{2,1,0:T(8,128)(2,1)} %bitcast.83), calls=%async_computation.1 | async-start | bytes 6291456 | tf_op jit(solution)/shard_map/all_to_all | solution.py:50
  48.0 2.2 mul.68
  50.2 4.9 %mul.69 = f32[1536,512]{1,0:T(8,128)} reshape(f32[384,4,512]{2,1,0:T(4,128)} %mul.68) | data formatting | bytes 6291456 | tf_op jit(solution)/shard_map/mul | solution.py:99
  55.1 44.7 %all-to-all-done.1 = bf16[8,384,512]{2,1,0:T(8,128)(2,1)} async-done(((bf16[8,384,512]{2,1,0:T(8,128)(2,1)}), bf16[8,384,512]{2,1,0:T(8,128)(2,1)}, u32[]{:S(2)}, u32[]{:S(2)}) %all-to-all-start.1) | async-done | bytes 3145760 | tf_op jit(solution)/shard_map/all_to_all | solution.py:50
  99.8 7.8 %gather_fusion.1 = bf16[1536,512]{1,0:T(8,128)(2,1)} fusion(bf16[3072,512]{1,0:T(8,128)(2,1)} %bitcast.7, s32[2048]{0:T(1024)S(1)} %pad_clamp_fusion), kind=kCustom, calls=%fused_computation.1 | custom fusion | bytes 3151872 | tf_op jit(solution)/shard_map/gather | solution.py:51
  107.6 3.5 %reshape.274 = bf16[384,4,512]{2,1,0:T(4,128)(2,1)} reshape(bf16[1536,512]{1,0:T(8,128)(2,1)} %gather_fusion.1) | data formatting | bytes 3145728 | tf_op jit(solution)/shard_map/reshape | solution.py:51
  111.1 2.8 fusion.18
  114.3 2.4 fusion.43
  116.8 34.0 %while.14 = (s32[]{:T(128)}, f32[384]{0:T(512)S(1)}, f32[384]{0:T(512)S(1)}, f32[384,512]{1,0:T(8,128)S(1)}, bf16[8,1024,512]{2,1,0:T(8,128)(2,1)}, /*index=5*/bf16[384,512]{1,0:T(8,128)(2,1)S(1)}, s32[]{:T(128)}) while((s32[]{:T(128)}, f32[384]{0:T(512)S(1)}, f32[384]{0:T(512)S(1)}, f32[384,512]{1,0:T(8,128)S(1)}, ...), condition=%wide.region_10.11_spmd, body=%wide.region_7.10_spmd.sunk | while | flops 808059648 | bytes 8806493 | solution.py:79
  121.1 2.0 fusion.59
  129.6 2.0 fusion.59
  133.8 2.0 fusion.59
  142.3 2.0 fusion.59
  151.2 10.7 %scatter_custom_fusion.1 = bf16[3072,512]{1,0:T(8,128)(2,1)} fusion(s32[1536]{0:T(1024)S(1)} %fusion.31, f32[1536,512]{1,0:T(8,128)} %mul.69, f32[]{:T(128)} %constant.84.clone.1, f32[1536]{0:T(1024)S(1)} %mul.66, bf16[]{:T(256)} %constant.87.clone.1), kind=kCustom, calls=%fused_computation.23 | custom fusion | flops 2359296 | bytes 6299654 | tf_op jit(solution)/shard_map/scatter | solution.py:104
  161.9 4.4 %all-to-all-start.2 = ((bf16[8,384,512]{2,1,0:T(8,128)(2,1)}), bf16[8,384,512]{2,1,0:T(8,128)(2,1)}, u32[]{:S(2)}, u32[]{:S(2)}) async-start(bf16[8,384,512]{2,1,0:T(8,128)(2,1)} %bitcast.82), calls=%async_computation.2 | async-start | bytes 6291456 | tf_op jit(solution)/shard_map/all_to_all | solution.py:106
  166.6 2.0 slice.22
  172.5 67.0 %psum.15 = f32[]{:T(128)} all-reduce(f32[]{:T(128)} %subtract_reduce_fusion), channel_id=1, replica_groups=mesh['dp'=4,'lib'=8] {'dp','lib'}, use_global_device_ids=true, to_apply=%region_16.17 | all-reduce | flops 1 | bytes 8 | tf_op jit(solution)/shard_map/psum | solution.py:114
  240.2 68.1 %all-reduce.2.cloned.1.call-done = f32[512,512]{0,1:T(8,128)} async-done(((f32[512,512]{0,1:T(8,128)}), f32[512,512]{0,1:T(8,128)}) %all-reduce.2.cloned.1.call-update) | async-done | bytes 1048592 | tf_op jit(solution)/shard_map/psum | solution.py:114
  308.2 2.5 copy.15
  310.7 23.2 %scatter_custom_fusion.2 = f32[2048,512]{1,0:T(8,128)} fusion(s32[3072]{0:T(1024)S(1)} %bitcast.88, bf16[3072,512]{1,0:T(8,128)(2,1)} %bitcast.19, f32[]{:T(128)} %constant.73.clone.1), kind=kCustom, calls=%fused_computation.19 | custom fusion | flops 3145728 | bytes 7340036 | tf_op jit(solution)/shard_map/scatter-add | solution.py:112
  (97 shorter events, 35.0 us)
Async XLA Ops:
  7.2 21.2 %copy-start = (bf16[2048,512]{1,0:T(8,128)(2,1)S(1)}, bf16[2048,512]{1,0:T(8,128)(2,1)}, u32[]{:S(2)}) copy-start(bf16[2048,512]{1,0:T(8,128)(2,1)} %param.11) | copy-start | bytes 6291460
  7.2 109.6 %all-gather.2.cloned.1.call-start = ((), (), s32[]{:S(2)}) async-start(), calls=%async_computation.3 | async-start | bytes 9437184 | tf_op jit(solution)/shard_map/all_gather | solution.py:73
  41.7 4.8 %copy-start.3 = (bf16[512,512]{1,0:T(8,128)(2,1)S(1)}, bf16[512,512]{1,0:T(8,128)(2,1)}, u32[]{:S(2)}) copy-start(bf16[512,512]{1,0:T(8,128)(2,1)} %param.9) | copy-start | bytes 1572868
  41.7 4.8 %copy-start.4 = (bf16[384,512]{1,0:T(8,128)(2,1)S(1)}, bf16[384,512]{1,0:T(8,128)(2,1)}, u32[]{:S(2)}) copy-start(bf16[384,512]{1,0:T(8,128)(2,1)} %param.8) | copy-start | bytes 1179652
  41.7 58.1 %all-to-all-start.1 = ((bf16[8,384,512]{2,1,0:T(8,128)(2,1)}), bf16[8,384,512]{2,1,0:T(8,128)(2,1)}, u32[]{:S(2)}, u32[]{:S(2)}) async-start(bf16[8,384,512]{2,1,0:T(8,128)(2,1)} %bitcast.83), calls=%async_computation.1 | async-start | bytes 6291456 | tf_op jit(solution)/shard_map/all_to_all | solution.py:50
  47.1 0.9 copy-start.1
  111.1 2.9 copy-start.6
  161.9 148.9 %all-to-all-start.2 = ((bf16[8,384,512]{2,1,0:T(8,128)(2,1)}), bf16[8,384,512]{2,1,0:T(8,128)(2,1)}, u32[]{:S(2)}, u32[]{:S(2)}) async-start(bf16[8,384,512]{2,1,0:T(8,128)(2,1)} %bitcast.82), calls=%async_computation.2 | async-start | bytes 6291456 | tf_op jit(solution)/shard_map/all_to_all | solution.py:106
  166.3 3.8 %copy-start.5 = (bf16[384,512]{1,0:T(8,128)(2,1)S(1)}, bf16[384,512]{1,0:T(8,128)(2,1)}, u32[]{:S(2)}) copy-start(bf16[384,512]{1,0:T(8,128)(2,1)} %param.8) | copy-start | bytes 1179652
  166.3 141.9 %all-reduce.2.cloned.1.call-start = ((), (), s32[]{:S(2)}) async-start(), calls=%async_computation.4 | async-start | bytes 2097152 | tf_op jit(solution)/shard_map/psum | solution.py:114
  166.6 3.5 %copy-start.2 = (f32[384,512]{1,0:T(8,128)S(1)}, f32[384,512]{1,0:T(8,128)}, u32[]{:S(2)}) copy-start(f32[384,512]{1,0:T(8,128)} %copy-done.1) | copy-start | bytes 2359300
Sparse Core Ops, SparseCore 0:
  9.9 81.2 all-gather.1
  172.9 135.2 all-reduce.1
where the time goes:
time: 343 us; the launch traced here: 342 us
  waiting for transfers between devices  113 us (33%)
  blocking collectives  77 us (22%)
  local copies, waits for them, and re-layouts  45.5 us (13%)
  other arithmetic  41.5 us (12%)
  matrix products  38.6 us (11%)
  between operations  16.1 us (5%)
  starting transfers between devices  9.51 us (3%)
    psum x1, waiting for transfers between devices, per_device(): grad_w, loss_sum = lax.psum((grad_local, loss_terms), ('dp', 'lib'))  68.1 us
    psum x1, blocking collectives, per_device(): grad_w, loss_sum = lax.psum((grad_local, loss_terms), ('dp', 'lib'))  67 us
    all_to_all x1, waiting for transfers between devices, per_device(): lax.all_to_all(fetched, 'lib', split_axis=0, concat_axis=0, tiled=True)  44.7 us
    scatter-add x1, other arithmetic, per_device(): grad_mol = jnp.zeros((mol_count, width), jnp.float32).at[received.reshape...  23.2 us
    dot_general x8, matrix products, absorb(): lax.dot_general(spectrum_encoding, block, (((1,), (1,)), ((), ())), prefe...  15.7 us
    dot_general x8, matrix products, absorb(): jnp.dot(weights.astype(jnp.bfloat16), block, preferred_element_type=jnp.f...  15.5 us
    gather x1, local copies, waits for them, and re-layouts, per_device(): fetched = mol_rows[received]  13.3 us
    scatter x1, other arithmetic, per_device(): outgoing = jnp.zeros((lib_size * capacity, width), jnp.bfloat16).at[posit...  10.7 us
  transfers between devices with their start and end apart: 4, of which 2 were waited for; matrix products, arithmetic and copies ran while one was open for 17% of the time, Pallas kernels for 0%

commit v1 on v0

v1 whole, which is shorter than its diff:
```python
import functools

import jax
import jax.numpy as jnp
from jax import lax
from jax.experimental import pallas as pl
from jax.experimental.pallas import tpu as pltpu
from jax.sharding import PartitionSpec as P


sharpness_divisor = 0.07
INV = 1.0 / sharpness_divisor
INV_LOG2 = 1.4426950408889634 / sharpness_divisor
BASE = 256
F32 = jnp.float32
BF16 = jnp.bfloat16
VMEM_BYTES = 24 * 1024 * 1024
ROOM_BYTES = 36 * 1024 * 1024
PIECES = 4


def nt(a, b):
    return lax.dot_general(a, b, (((1,), (1,)), ((), ())), preferred_element_type=F32)


def nn(a, b):
    return lax.dot_general(a, b, (((1,), (0,)), ((), ())), preferred_element_type=F32)


def tree(terms):
    while len(terms) > 1:
        terms = [a + b for a, b in zip(terms[::2], terms[1::2])]
    return terms[0]


def turn_kernel(bank_ref, mol_ref, bankt_ref, molt_ref):
    for src, dst in ((bank_ref, bankt_ref), (mol_ref, molt_ref)):
        for r in range(0, src.shape[0], 256):
            dst[:, r : r + 256] = src[r : r + 256, :].T


def score_kernel(rows, lanes, mol_tile, at_lane, aliased, *refs):
    own_ref, xa_ref, xb_ref, w_ref, bank_ref, mol_ref = refs[:6]
    refs = refs[6 + aliased :]
    qt_ref, sp_ref, wbt_ref, st_ref, lse_ref, bs_ref, wt_ref = refs
    mol_count = mol_ref.shape[0]
    pair = 2 * rows
    sp_ref[at_lane : at_lane + rows, :] = xa_ref[:rows, :]
    sp_ref[at_lane + rows : at_lane + pair, :] = xb_ref[:rows, :]
    wt_ref[...] = w_ref[...].T
    digits = jnp.concatenate(
        [xa_ref[rows : rows + 16, :rows].astype(F32), xb_ref[rows : rows + 16, :rows].astype(F32)],
        axis=1,
    )
    base = (own_ref[0] * mol_count).astype(F32)
    local = digits[0:4] * BASE + digits[4:8] - base
    local = jnp.where((local >= 0) & (local < mol_count), local, -1.0)
    for c in range(0, pair, lanes):
        cols = slice(c, c + lanes)
        out = slice(at_lane + c, at_lane + c + lanes)
        ut = nt(wt_ref[...], sp_ref[out, :])
        norm = jnp.sqrt(jnp.sum(ut * ut, axis=0, keepdims=True) + 1e-06)
        qt = (ut * (1.0 / norm)).astype(BF16)
        qt_ref[:, out] = qt
        here_at = local[:, cols]
        at = here_at.astype(jnp.int32)
        at = jnp.concatenate([at, at], axis=0)
        group = at >> 3
        within = at & 7
        picked = jnp.zeros((8, lanes), F32)
        for start in range(0, mol_count, mol_tile):
            s = nn(mol_ref[start : start + mol_tile, :], qt)
            for r in range(0, mol_tile, 8):
                taken = jnp.take_along_axis(s[r : r + 8], within, axis=0)
                picked = jnp.where(group == (start + r) // 8, taken, picked)
        cs = picked[0:4]
        d = nn(bank_ref[...], qt)
        bs_ref[:, cols] = d
        masked = jnp.where(here_at >= 0, cs, -1e30)
        best = jnp.maximum(
            jnp.max(d, axis=0, keepdims=True), jnp.max(masked, axis=0, keepdims=True)
        )
        total = jnp.sum(jnp.exp2((masked - best) * INV_LOG2), axis=0, keepdims=True)
        e = jnp.exp2((bs_ref[:, cols] - best) * INV_LOG2)
        wbt_ref[:, out] = e.astype(BF16)
        total = total + jnp.sum(e, axis=0, keepdims=True)
        zero = jnp.zeros((1, lanes), F32)
        sent = jnp.concatenate(
            [best * INV + jnp.log(total), jnp.where(here_at[0:1] >= 0, cs[0:1] * INV, 0.0)], axis=0
        )
        lse_ref[:, out] = sent
        st_ref[:, out] = jnp.concatenate(
            [best * INV, zero, zero, zero, cs * INV, here_at, norm, zero, zero, zero], axis=0
        )


def bank_kernel(whole, pair, bankt_ref, wbt_ref, acc_ref):
    cols = pl.ds(pl.multiple_of(pl.program_id(0) * pair, 256), pair) if whole else slice(None)
    acc_ref[:, cols] = nn(bankt_ref[...], wbt_ref[:, cols])


def grad_kernel(rows, lanes, whole, lib_size, mine_ref, *refs):
    lse_refs = refs[:lib_size]
    st_ref, qt_ref, sp_ref, acc_ref, molt_ref = refs[lib_size : lib_size + 5]
    refs = refs[lib_size + 5 :]
    gt_ref, loss_ref = refs[:2]
    gw_refs = refs[2 : 2 + lib_size]
    dq_ref, gwt_ref, block_ref = refs[-3:]
    p = pl.program_id(0)
    last = pl.num_programs(0) - 1
    pair = 2 * rows
    mol_count = molt_ref.shape[1]
    start = pl.multiple_of(p * pair, 256) if whole else 0
    here = pl.ds(start, pair)
    parts = []
    for m in range(lib_size):
        r = lse_refs[m][:, pl.ds(pl.multiple_of((p ^ (m >> 1)) * pair, 256), pair)]
        if m & 1:
            r = jnp.concatenate([r[:, rows:], r[:, :rows]], axis=1)
        parts.append(r)
    top = parts[0][0:1]
    for r in parts[1:]:
        top = jnp.maximum(top, r[0:1])
    total = tree([jnp.exp(r[0:1] - top) for r in parts])
    cs0 = tree([r[1:2] for r in parts])
    lse = top + jnp.log(total)
    terms = lse - cs0
    for half in range(2):
        block_ref[pl.ds(2 * p + half, 1), :] = jnp.broadcast_to(
            jnp.sum(terms[:, half * rows : (half + 1) * rows]), (1, block_ref.shape[1])
        )

    st = st_ref[:, here]
    inv_norm = 1.0 / st[12:13]
    at = [st[8 + j : 9 + j].astype(jnp.int32) for j in range(4)]
    g = []
    for j in range(4):
        e = jnp.exp(st[4 + j : 5 + j] - lse)
        g.append(jnp.where(at[j] >= 0, e - (1.0 if j == 0 else 0.0), 0.0))
    for j in range(1, 4):
        for k in range(j):
            same = (at[j] == at[k]) & (at[j] >= 0)
            g[k] = g[k] + jnp.where(same, g[j], 0.0)
            at[j] = jnp.where(same, -1, at[j])
    row = lax.broadcasted_iota(jnp.int16, (16, lanes), 0)
    for c in range(0, pair, lanes):
        cols = slice(c, c + lanes)
        out = pl.ds(start + c, lanes)
        gap = [
            jnp.broadcast_to(at[j][:, cols], (16, lanes)).astype(jnp.int16) - row for j in range(4)
        ]
        put = [jnp.broadcast_to(g[j][:, cols], (16, lanes)).astype(BF16) for j in range(4)]
        for r in range(0, mol_count, 16):
            w = jnp.zeros((16, lanes), BF16)
            for j in range(4):
                w = jnp.where(gap[j] == jnp.int16(r), put[j], w)
            gt_ref[r : r + 16, out] = w
        dq_ref[:, cols] = nn(molt_ref[...], gt_ref[:, out])
    scale = jnp.exp(st[0:1] - lse)
    dq = dq_ref[...] + acc_ref[:, here] * scale
    unit = qt_ref[:, here].astype(F32)
    along = jnp.sum(unit * dq, axis=0, keepdims=True)
    du = ((dq - unit * along) * (inv_norm * INV)).astype(BF16)
    part = nn(du, sp_ref[here, :])

    @pl.when(p == 0)
    def _():
        gwt_ref[...] = jnp.zeros_like(gwt_ref)

    gwt_ref[...] += part

    if not whole:
        gm_ref = refs[2 + lib_size]

        @pl.when(p == 0)
        def _():
            gm_ref[...] = jnp.zeros_like(gm_ref)

        gm_ref[...] += nt(gt_ref[...], qt_ref[...]) * INV

    @pl.when(p == last)
    def _():
        gwt_ref[...] = gwt_ref[...].T
        for m in range(lib_size):
            chunk = gw_refs[m].shape[0]
            start = pl.multiple_of((mine_ref[0] ^ m) * chunk, chunk)
            gw_refs[m][...] = gwt_ref[pl.ds(start, chunk), :].astype(BF16)
        left = jnp.broadcast_to(
            tree([block_ref[m : m + 1, :] for m in range(lib_size)]), (16, block_ref.shape[1])
        )
        split = []
        for _ in range(3):
            part_of = left.astype(BF16).astype(F32)
            split.append(part_of)
            left = left - part_of
        spot = lax.broadcasted_iota(jnp.int32, left.shape, 0)
        row = jnp.where(spot == 0, split[0], jnp.where(spot == 1, split[1], split[2]))
        loss_ref[...] = jnp.where(spot < 3, row, 0.0).astype(BF16)


def mol_kernel(first, gt_ref, qt_ref, *refs):
    out_ref = refs[-1]
    out_ref[...] = nt(gt_ref[first : first + out_ref.shape[0], :], qt_ref[...]) * INV


def fold_kernel(loss_ref, *refs):
    out_ref = refs[-1]
    chunk = refs[0].shape[0]
    out_ref[:chunk, :] = tree([r[...].astype(F32) for r in refs[:-1]]).astype(BF16)
    out_ref[chunk:, :] = loss_ref[...]


def share_kernel(*refs):
    out_ref, loss_ref = refs[-2:]
    chunk = out_ref.shape[0]
    total = tree([r[...].astype(F32) for r in refs[:-2]])
    out_ref[...] = total[:chunk].astype(BF16)
    loss = total[chunk : chunk + 1] + total[chunk + 1 : chunk + 2] + total[chunk + 2 : chunk + 3]
    loss_ref[...] = jnp.broadcast_to(loss[:, :128], loss_ref.shape)


def place_kernel(mine_ref, *refs):
    out_ref = refs[-1]
    for m, r in enumerate(refs[:-1]):
        start = pl.multiple_of((mine_ref[0] ^ m) * r.shape[0], r.shape[0])
        out_ref[pl.ds(start, r.shape[0]), :] = r[...].astype(F32)


def params(limit=VMEM_BYTES, **kw):
    return pltpu.CompilerParams(vmem_limit_bytes=limit, **kw)


def cost(flops, nbytes):
    return pl.CostEstimate(flops=flops, bytes_accessed=nbytes, transcendentals=0)


def per_device(spectra, w_proj, fixed_library_matrix, mol_rows, cand_ids, iso_count):
    rows, width = spectra.shape
    mol_count = mol_rows.shape[0]
    bank_count = fixed_library_matrix.shape[0]
    lib_size = lax.axis_size("lib")
    dp_size = lax.axis_size("dp")
    columns = cand_ids.shape[1]
    pairs = lib_size // 2
    pair = 2 * rows
    n = pairs * pair
    me = lax.axis_index("lib").astype(jnp.int32)[None]
    full = pl.BlockSpec(memory_space=pltpu.VMEM)
    smem = pl.BlockSpec(memory_space=pltpu.SMEM)
    anywhere = pl.BlockSpec(memory_space=pl.ANY)
    sds = jax.ShapeDtypeStruct
    held = n * (2 * width + 2 * width + 2 * mol_count + 2 * bank_count + 4 * width)
    whole = held <= ROOM_BYTES

    column = jnp.arange(columns, dtype=jnp.int32)[:, None]
    ids = cand_ids.T % (lib_size * mol_count)
    dead = column > iso_count[None, :]
    high = jnp.where(dead, -1, ids // BASE)
    low = ids % BASE
    digits = jnp.concatenate([high, low], axis=0).astype(BF16)
    digits = jnp.pad(digits, ((0, 16 - 2 * columns), (0, width - rows)))
    own = jnp.concatenate([spectra, digits], axis=0)
    own, me = lax.optimization_barrier((own, me))

    def swap(x, mask):
        return lax.ppermute(x, "lib", [(i, i ^ mask) for i in range(lib_size)])

    blocks = [own] + [None] * (lib_size - 1)
    for k in range(2, lib_size, 2):
        blocks[k] = swap(own, k)
    blocks[1] = swap(own, 1)
    for k in range(2, lib_size, 2):
        blocks[k + 1] = swap(blocks[k], 1)

    outs = [
        ((width, n), BF16, (width, pair), lambda p: (0, p)),
        ((n, width), BF16, (pair, width), lambda p: (p, 0)),
        ((bank_count, n), BF16, (bank_count, pair), lambda p: (0, p)),
        ((16, n), F32, (16, pair), lambda p: (0, p)),
        ((2, n), F32, (2, pair), lambda p: (0, p)),
    ]
    spec_q, spec_s, spec_w, spec_st = [full if whole else pl.BlockSpec(b, f) for _, _, b, f in outs[:4]]
    spec_acc = spec_q
    state = []
    for p in range(pairs):
        state = pl.pallas_call(
            functools.partial(score_kernel, rows, 256, 1024, p * pair if whole else 0, len(state)),
            grid=(1,),
            in_specs=[smem] + [full] * 5 + [anywhere] * len(state),
            out_specs=[
                full if whole else pl.BlockSpec(b, functools.partial(lambda f, p, i: f(p), f, p))
                for _, _, b, f in outs
            ],
            out_shape=[sds(s, d) for s, d, _, _ in outs],
            scratch_shapes=[pltpu.VMEM((bank_count, pair), F32), pltpu.VMEM((width, width), BF16)],
            input_output_aliases={6 + i: i for i in range(len(state))},
            compiler_params=params(),
            cost_estimate=cost(2 * pair * width * (width + bank_count + mol_count), 8 << 20),
            name="score",
        )(me, blocks[2 * p], blocks[2 * p + 1], w_proj, fixed_library_matrix, mol_rows, *state)
    q_t, spec_all, wb_t, st, lse_own = state

    lse_all = [lse_own] + [swap(lse_own, m) for m in range(1, lib_size)]

    bank_t, mol_t = pl.pallas_call(
        turn_kernel,
        in_specs=[full] * 2,
        out_specs=[full] * 2,
        out_shape=[sds((a.shape[1], a.shape[0]), BF16) for a in (fixed_library_matrix, mol_rows)],
        compiler_params=params(),
        cost_estimate=cost(0, 8 << 20),
        name="turn",
    )(fixed_library_matrix, mol_rows)

    acc = pl.pallas_call(
        functools.partial(bank_kernel, whole, pair),
        grid=(pairs,),
        in_specs=[full, spec_w],
        out_specs=spec_acc,
        out_shape=sds((width, n), F32),
        compiler_params=params(),
        cost_estimate=cost(2 * n * width * bank_count, 14 << 20),
        name="bank",
    )(bank_t, wb_t)

    chunk = width // lib_size
    grad_outs = [sds((mol_count, n if whole else pair), BF16), sds((16, width), BF16)]
    grad_outs += [sds((chunk, width), BF16)] * lib_size
    if not whole:
        grad_outs.append(sds((mol_count, width), F32))
    grads = pl.pallas_call(
        functools.partial(grad_kernel, rows, 256, whole, lib_size),
        grid=(pairs,),
        in_specs=[smem] + [full] * lib_size + [spec_st, spec_q, spec_s, spec_acc, full],
        out_specs=[full] * len(grad_outs),
        out_shape=grad_outs,
        scratch_shapes=[
            pltpu.VMEM((width, pair), F32),
            pltpu.VMEM((width, width), F32),
            pltpu.VMEM((lib_size, width), F32),
        ],
        compiler_params=params() if whole else params(40 << 20),
        cost_estimate=cost(2 * n * width * (mol_count + width), 24 << 20),
        name="grad",
    )(me, *lse_all, st, q_t, spec_all, acc, mol_t)
    g_t, loss_part = grads[:2]
    gw_parts = grads[2 : 2 + lib_size]

    if whole:
        piece = mol_count // PIECES
        grad_mol = []
        for r in range(PIECES):
            grad_mol = [
                pl.pallas_call(
                    functools.partial(mol_kernel, r * piece),
                    grid=(1,),
                    in_specs=[full, full] + [anywhere] * len(grad_mol),
                    out_specs=pl.BlockSpec((piece, width), functools.partial(lambda r, i: (r, 0), r)),
                    out_shape=pltpu.HBM((mol_count, width), F32),
                    input_output_aliases={2: 0} if grad_mol else {},
                    compiler_params=params(),
                    cost_estimate=cost(2 * n * width * piece, 7 << 20),
                    name="mol",
                )(g_t, q_t, *[pltpu.with_memory_space_constraint(x, pltpu.HBM) for x in grad_mol])
            ]
        grad_mol = grad_mol[0]
    else:
        grad_mol = grads[-1]

    got = [gw_parts[0]] + [swap(gw_parts[m], m) for m in range(1, lib_size)]
    sent = pl.pallas_call(
        fold_kernel,
        in_specs=[full] * (1 + lib_size),
        out_specs=full,
        out_shape=sds((chunk + 16, width), BF16),
        compiler_params=params(8 << 20),
        cost_estimate=cost(0, 1 << 20),
        name="fold",
    )(loss_part, *got)
    terms = [sent]
    for k in range(1, dp_size):
        terms.append(lax.ppermute(sent, "dp", [(i, i ^ k) for i in range(dp_size)]))
    shared, loss_sum = pl.pallas_call(
        share_kernel,
        in_specs=[full] * dp_size,
        out_specs=[full, full],
        out_shape=[sds((chunk, width), BF16), sds((8, 128), F32)],
        compiler_params=params(8 << 20),
        cost_estimate=cost(0, 1 << 20),
        name="share",
    )(*terms)
    everyone = [shared] + [swap(shared, m) for m in range(1, lib_size)]
    grad_w = pl.pallas_call(
        place_kernel,
        in_specs=[smem] + [full] * lib_size,
        out_specs=full,
        out_shape=pltpu.HBM((width, width), F32),
        compiler_params=params(8 << 20),
        cost_estimate=cost(0, 2 << 20),
        name="place",
    )(me, *everyone)
    loss = loss_sum[0, 0] / (rows * dp_size * lib_size)
    return (grad_w, grad_mol, loss)


def solution(mesh):
    placed = (
        P(("dp", "lib"), None),
        P(),
        P("lib", None),
        P(("dp", "lib"), None),
        P(("dp", "lib"), None),
        P(("dp", "lib")),
    )

    return jax.shard_map(
        per_device,
        mesh=mesh,
        in_specs=placed,
        out_specs=(P(), P(("dp", "lib"), None), P()),
        check_vma=False,
    )
```

time: 343 us -> 111 us (0.32)
  waiting for transfers between devices: 113 us -> 23.5 us
  blocking collectives: 77 us -> 0 us
  Pallas kernels: 0 us -> 50.2 us
  local copies, waits for them, and re-layouts: 45.5 us -> 4.38 us
  other arithmetic: 41.5 us -> 1.77 us
  matrix products: 38.6 us -> 0 us
  starting transfers between devices: 9.51 us -> 28.6 us
  between operations: 16.1 us -> 2.63 us
    psum x1 -> x0, waiting for transfers between devices: 68.1 us -> none  [per_device(): grad_w, loss_sum = lax.psum((grad_local, loss_terms), ('dp', 'lib'))]
    psum x1 -> x0, blocking collectives: 67 us -> none  [per_device(): grad_w, loss_sum = lax.psum((grad_local, loss_terms), ('dp', 'lib'))]
    pallas_call x0 -> x14, Pallas kernels: none -> 50.2 us  [the longest x4 17.7 us: per_device(): pl.pallas_call(functools.partial(score_kernel, rows, 256, 1024, p * pair...]
    all_to_all x2 -> x0, waiting for transfers between devices: 44.7 us -> none  [the longest x1 44.7 us: per_device(): lax.all_to_all(fetched, 'lib', split_axis=0, concat_axis=0, tiled=True)]
    dot_general x20 -> x0, matrix products: 38.6 us -> none  [the longest x8 15.7 us: absorb(): lax.dot_general(spectrum_encoding, block, (((1,), (1,)), ((), ())), prefe...]
    ppermute x0 -> x31, starting transfers between devices: none -> 28.6 us  [the longest x28 24.1 us: swap(): return lax.ppermute(x, 'lib', [(i, i ^ mask) for i in range(lib_size)])]
    ppermute x0 -> x31, waiting for transfers between devices: none -> 23.5 us  [the longest x28 19.6 us: swap(): return lax.ppermute(x, 'lib', [(i, i ^ mask) for i in range(lib_size)])]
    scatter-add x1 -> x0, other arithmetic: 23.2 us -> none  [per_device(): grad_mol = jnp.zeros((mol_count, width), jnp.float32).at[received.reshape...]
  transfers between devices with their start and end apart: 4 -> 31, of which waited for: 2 -> 5; matrix products, arithmetic and copies ran while one was open for 17% -> 0% of each run, Pallas kernels for 0% -> 26%
where the time goes in v1:
time: 111 us
  Pallas kernels  50.2 us (45%)
  starting transfers between devices  28.6 us (26%)
  waiting for transfers between devices  23.5 us (21%)
  local copies, waits for them, and re-layouts  4.38 us (4%)
  between operations  2.63 us (2%)
  other arithmetic  1.77 us (2%)
    ppermute x28, starting transfers between devices, swap(): return lax.ppermute(x, 'lib', [(i, i ^ mask) for i in range(lib_size)])  24.1 us
    ppermute x28, waiting for transfers between devices, swap(): return lax.ppermute(x, 'lib', [(i, i ^ mask) for i in range(lib_size)])  19.6 us
    pallas_call x4, Pallas kernels, per_device(): pl.pallas_call(functools.partial(score_kernel, rows, 256, 1024, p * pair...  17.7 us
    pallas_call x1, Pallas kernels, per_device(): pl.pallas_call(functools.partial(grad_kernel, rows, 256, whole, lib_size)...  15.2 us
    pallas_call x4, Pallas kernels, per_device(): pl.pallas_call(functools.partial(mol_kernel, r * piece), grid=(1,), in_sp...  11.2 us
    ppermute x3, starting transfers between devices, per_device(): terms.append(lax.ppermute(sent, 'dp', [(i, i ^ k) for i in range(dp_size)]))  4.45 us
    pallas_call x1, Pallas kernels, per_device(): pl.pallas_call(functools.partial(bank_kernel, whole, pair), grid=(pairs,)...  4.02 us
    unnamed x12, local copies, waits for them, and re-layouts  3.87 us
  transfers between devices with their start and end apart: 31, of which 5 were waited for; matrix products, arithmetic and copies ran while one was open for 0% of the time, Pallas kernels for 26%

profile of v1, /device:TPU:0, one launch (start us, length us, event | category | flops | bytes accessed | tf_op | source)
XLA Modules:
  0.0 111.1 jit_solution(1574912569800575856)
XLA Ops:
  2.4 3.0 %collective-permute-start.4 = (bf16[400,512]{1,0:T(8,128)(2,1)S(1)}, bf16[400,512]{1,0:T(8,128)(2,1)S(1)}, u32[]{:S(2)}, u32[]{:S(2)}) collective-permute-start(bf16[400,512]{1,0:T(8,128)(2,1)S(1)} %pad_maximum_fusion.refs_1_), channel_id=1, source_target_pairs={{0,2},{1,3},{2,0},{3,1},{4,6},{5,7},{6,4},{7,5},{8,10},{9,11},{10,... | collective-permute-start | bytes 1228808 | tf_op jit(solution)/shard_map/ppermute | solution.py:266
  5.4 1.5 %collective-permute-start.2 = (bf16[400,512]{1,0:T(8,128)(2,1)S(1)}, bf16[400,512]{1,0:T(8,128)(2,1)S(1)}, u32[]{:S(2)}, u32[]{:S(2)}) collective-permute-start(bf16[400,512]{1,0:T(8,128)(2,1)S(1)} %pad_maximum_fusion.refs_1_), channel_id=1, source_target_pairs={{0,4},{1,5},{2,6},{3,7},{4,0},{5,1},{6,2},{7,3},{8,12},{9,13},{10,... | collective-permute-start | bytes 1228808 | tf_op jit(solution)/shard_map/ppermute | solution.py:266
  7.0 8.8 %collective-permute-done.4.refs_1_ = bf16[400,512]{1,0:T(8,128)(2,1)S(1)} collective-permute-done((bf16[400,512]{1,0:T(8,128)(2,1)S(1)}, bf16[400,512]{1,0:T(8,128)(2,1)S(1)}, u32[]{:S(2)}, u32[]{:S(2)}) %collective-permute-start.4) | collective-permute-done | bytes 409632 | tf_op jit(solution)/shard_map/ppermute | solution.py:266
  15.8 9.4 %collective-permute-done.2.refs_1_ = bf16[400,512]{1,0:T(8,128)(2,1)S(1)} collective-permute-done((bf16[400,512]{1,0:T(8,128)(2,1)S(1)}, bf16[400,512]{1,0:T(8,128)(2,1)S(1)}, u32[]{:S(2)}, u32[]{:S(2)}) %collective-permute-start.2) | collective-permute-done | bytes 409632 | tf_op jit(solution)/shard_map/ppermute | solution.py:266
  25.7 1.6 %copy-done = bf16[2048,512]{1,0:T(8,128)(2,1)S(1)} copy-done((bf16[2048,512]{1,0:T(8,128)(2,1)S(1)}, bf16[2048,512]{1,0:T(8,128)(2,1)}, u32[]{:S(2)}) %copy-start) | copy-done | bytes 2097176
  29.5 4.4 %score.4 = (bf16[512,3072]{1,0:T(8,128)(2,1)S(1)}, bf16[3072,512]{1,0:T(8,128)(2,1)S(1)}, bf16[1024,3072]{1,0:T(8,128)(2,1)S(1)}, f32[16,3072]{1,0:T(8,128)S(1)}, f32[2,3072]{1,0:T(2,128)S(1)}) custom-call(s32[1]{0:T(128)} %bitcast.1.refs_0_.mine_ref, bf16[400,512]{1,0:T(8,128)(2,1)S(1)} %pad_maximum_fusion.refs_1_, ...), custom_call_target="tpu_custom_call" | custom-call | flops 2818572288 | bytes 8388608 | tf_op jit(solution)/shard_map/score/pallas_call | solution.py:286
  33.9 4.4 %score.5 = (bf16[512,3072]{1,0:T(8,128)(2,1)S(1)}, bf16[3072,512]{1,0:T(8,128)(2,1)S(1)}, bf16[1024,3072]{1,0:T(8,128)(2,1)S(1)}, f32[16,3072]{1,0:T(8,128)S(1)}, f32[2,3072]{1,0:T(2,128)S(1)}) custom-call(s32[1]{0:T(128)} %bitcast.1.refs_0_.mine_ref, ...), custom_call_target="tpu_custom_call", output_to_operand_aliasing={{0}: (6, {}), {1}: (7, {}), {2}: (8, {}), {3}: (9, {}), {4}... | custom-call | flops 2818572288 | bytes 8388608 | tf_op jit(solution)/shard_map/score/pallas_call | solution.py:286
  38.3 4.4 %score.6 = (bf16[512,3072]{1,0:T(8,128)(2,1)S(1)}, bf16[3072,512]{1,0:T(8,128)(2,1)S(1)}, bf16[1024,3072]{1,0:T(8,128)(2,1)S(1)}, f32[16,3072]{1,0:T(8,128)S(1)}, f32[2,3072]{1,0:T(2,128)S(1)}) custom-call(s32[1]{0:T(128)} %bitcast.1.refs_0_.mine_ref, ...), custom_call_target="tpu_custom_call", output_to_operand_aliasing={{0}: (6, {}), {1}: (7, {}), {2}: (8, {}), {3}: (9, {}), {4}... | custom-call | flops 2818572288 | bytes 8388608 | tf_op jit(solution)/shard_map/score/pallas_call | solution.py:286
  42.7 4.6 %score.7 = (bf16[512,3072]{1,0:T(8,128)(2,1)S(1)}, bf16[3072,512]{1,0:T(8,128)(2,1)S(1)}, bf16[1024,3072]{1,0:T(8,128)(2,1)S(1)}, f32[16,3072]{1,0:T(8,128)S(1)}, f32[2,3072]{1,0:T(2,128)S(1)}) custom-call(s32[1]{0:T(128)} %bitcast.1.refs_0_.mine_ref, ...), custom_call_target="tpu_custom_call", output_to_operand_aliasing={{0}: (6, {}), {1}: (7, {}), {2}: (8, {}), {3}: (9, {}), {4}... | custom-call | flops 2818572288 | bytes 8388608 | tf_op jit(solution)/shard_map/score/pallas_call | solution.py:286
  47.3 1.6 %collective-permute-start.10 = (f32[2,3072]{1,0:T(2,128)S(1)}, f32[2,3072]{1,0:T(2,128)S(1)}, u32[]{:S(2)}, u32[]{:S(2)}) collective-permute-start(f32[2,3072]{1,0:T(2,128)S(1)} %get-tuple-element.56.refs_0_), channel_id=1, source_target_pairs={{0,4},{1,5},{2,6},{3,7},{4,0},{5,1},{6,2},{7,3},{8,12},{9,13},{10,... | collective-permute-start | bytes 73736 | tf_op jit(solution)/shard_map/ppermute | solution.py:266
  49.8 1.4 %collective-permute-start.12 = (f32[2,3072]{1,0:T(2,128)S(1)}, f32[2,3072]{1,0:T(2,128)S(1)}, u32[]{:S(2)}, u32[]{:S(2)}) collective-permute-start(f32[2,3072]{1,0:T(2,128)S(1)} %get-tuple-element.56.refs_0_), channel_id=1, source_target_pairs={{0,6},{1,7},{2,4},{3,5},{4,2},{5,3},{6,0},{7,1},{8,14},{9,15},{10,... | collective-permute-start | bytes 73736 | tf_op jit(solution)/shard_map/ppermute | solution.py:266
  51.2 1.5 %collective-permute-start.13 = (f32[2,3072]{1,0:T(2,128)S(1)}, f32[2,3072]{1,0:T(2,128)S(1)}, u32[]{:S(2)}, u32[]{:S(2)}) collective-permute-start(f32[2,3072]{1,0:T(2,128)S(1)} %get-tuple-element.56.refs_0_), channel_id=1, source_target_pairs={{0,7},{1,6},{2,5},{3,4},{4,3},{5,2},{6,1},{7,0},{8,15},{9,14},{10,... | collective-permute-start | bytes 73736 | tf_op jit(solution)/shard_map/ppermute | solution.py:266
  54.6 4.0 %bank.1.refs_11_ = f32[512,3072]{1,0:T(8,128)S(1)} custom-call(bf16[512,1024]{1,0:T(8,128)(2,1)S(1)} %get-tuple-element.60.bankt_ref, bf16[1024,3072]{1,0:T(8,128)(2,1)S(1)} %get-tuple-element.61.wbt_ref), custom_call_target="tpu_custom_call" | custom-call | flops 3221225472 | bytes 14680064 | tf_op jit(solution)/shard_map/bank/pallas_call | solution.py:315
  58.7 15.2 %grad.1 = (bf16[2048,3072]{1,0:T(8,128)(2,1)S(1)}, bf16[16,512]{1,0:T(8,128)(2,1)S(1)}, bf16[64,512]{1,0:T(8,128)(2,1)S(1)}, bf16[64,512]{1,0:T(8,128)(2,1)S(1)}...) custom-call(s32[1]{0:T(128)} %bitcast.1.refs_0_.mine_ref, ...), custom_call_target="tpu_custom_call" | custom-call | flops 8053063680 | bytes 25165824 | tf_op jit(solution)/shard_map/grad/pallas_call | solution.py:331
  75.9 1.5 %collective-permute-start.17 = (bf16[64,512]{1,0:T(8,128)(2,1)S(1)}, bf16[64,512]{1,0:T(8,128)(2,1)S(1)}, u32[]{:S(2)}, u32[]{:S(2)}) collective-permute-start(bf16[64,512]{1,0:T(8,128)(2,1)S(1)} %get-tuple-element.68), channel_id=1, source_target_pairs={{0,4},{1,5},{2,6},{3,7},{4,0},{5,1},{6,2},{7,3},{8,12},{9,13},{10,... | collective-permute-start | bytes 196616 | tf_op jit(solution)/shard_map/ppermute | solution.py:266
  80.3 2.8 %mol.4.refs_0_ = f32[2048,512]{1,0:T(8,128)} custom-call(bf16[2048,3072]{1,0:T(8,128)(2,1)S(1)} %get-tuple-element.73.gt_ref, bf16[512,3072]{1,0:T(8,128)(2,1)S(1)} %get-tuple-element.58.refs_9_.qt_ref), custom_call_target="tpu_custom_call" | custom-call | flops 1610612736 | bytes 7340032 | tf_op jit(solution)/shard_map/mol/pallas_call | solution.py:354
  84.6 1.6 %collective-permute-start.21 = (bf16[80,512]{1,0:T(8,128)(2,1)S(1)}, bf16[80,512]{1,0:T(8,128)(2,1)S(1)}, u32[]{:S(2)}, u32[]{:S(2)}) collective-permute-start(bf16[80,512]{1,0:T(8,128)(2,1)S(1)} %fold.1.refs_0_), channel_id=1, source_target_pairs={{0,8},{8,0},{16,24},{24,16},{1,9},{9,1},{17,25},{25,17},{2,10},{10... | collective-permute-start | bytes 245768 | tf_op jit(solution)/shard_map/ppermute | solution.py:382
  86.2 2.6 %collective-permute-start.22 = (bf16[80,512]{1,0:T(8,128)(2,1)S(1)}, bf16[80,512]{1,0:T(8,128)(2,1)S(1)}, u32[]{:S(2)}, u32[]{:S(2)}) collective-permute-start(bf16[80,512]{1,0:T(8,128)(2,1)S(1)} %fold.1.refs_0_), channel_id=1, source_target_pairs={{0,16},{8,24},{16,0},{24,8},{1,17},{9,25},{17,1},{25,9},{2,18},{10... | collective-permute-start | bytes 245768 | tf_op jit(solution)/shard_map/ppermute | solution.py:382
  89.0 2.8 %mol.5.refs_0_ = f32[2048,512]{1,0:T(8,128)} custom-call(bf16[2048,3072]{1,0:T(8,128)(2,1)S(1)} %get-tuple-element.73.gt_ref, bf16[512,3072]{1,0:T(8,128)(2,1)S(1)} %get-tuple-element.58.refs_9_.qt_ref, f32[2048,512]{1,0:T(8,128)} %mol.4.refs_0_), custom_call_target="tpu_custom_call", output_to_operand_aliasing={{}: (2, {})} | custom-call | flops 1610612736 | bytes 7340032 | tf_op jit(solution)/shard_map/mol/pallas_call | solution.py:354
  91.8 3.9 %collective-permute-done.22.refs_2_ = bf16[80,512]{1,0:T(8,128)(2,1)S(1)} collective-permute-done((bf16[80,512]{1,0:T(8,128)(2,1)S(1)}, bf16[80,512]{1,0:T(8,128)(2,1)S(1)}, u32[]{:S(2)}, u32[]{:S(2)}) %collective-permute-start.22) | collective-permute-done | bytes 81952 | tf_op jit(solution)/shard_map/ppermute | solution.py:382
  95.8 1.5 %collective-permute-start.25 = (bf16[64,512]{1,0:T(8,128)(2,1)S(1)}, bf16[64,512]{1,0:T(8,128)(2,1)S(1)}, u32[]{:S(2)}, u32[]{:S(2)}) collective-permute-start(bf16[64,512]{1,0:T(8,128)(2,1)S(1)} %get-tuple-element.72.refs_0_), channel_id=1, source_target_pairs={{0,2},{1,3},{2,0},{3,1},{4,6},{5,7},{6,4},{7,5},{8,10},{9,11},{10,... | collective-permute-start | bytes 196616 | tf_op jit(solution)/shard_map/ppermute | solution.py:266
  97.3 2.8 %mol.6.refs_0_ = f32[2048,512]{1,0:T(8,128)} custom-call(bf16[2048,3072]{1,0:T(8,128)(2,1)S(1)} %get-tuple-element.73.gt_ref, bf16[512,3072]{1,0:T(8,128)(2,1)S(1)} %get-tuple-element.58.refs_9_.qt_ref, f32[2048,512]{1,0:T(8,128)} %mol.5.refs_0_), custom_call_target="tpu_custom_call", output_to_operand_aliasing={{}: (2, {})} | custom-call | flops 1610612736 | bytes 7340032 | tf_op jit(solution)/shard_map/mol/pallas_call | solution.py:354
  102.2 1.6 %collective-permute-start.29 = (bf16[64,512]{1,0:T(8,128)(2,1)S(1)}, bf16[64,512]{1,0:T(8,128)(2,1)S(1)}, u32[]{:S(2)}, u32[]{:S(2)}) collective-permute-start(bf16[64,512]{1,0:T(8,128)(2,1)S(1)} %get-tuple-element.72.refs_0_), channel_id=1, source_target_pairs={{0,6},{1,7},{2,4},{3,5},{4,2},{5,3},{6,0},{7,1},{8,14},{9,15},{10,... | collective-permute-start | bytes 196616 | tf_op jit(solution)/shard_map/ppermute | solution.py:266
  104.9 2.8 %mol.7 = f32[2048,512]{1,0:T(8,128)} custom-call(bf16[2048,3072]{1,0:T(8,128)(2,1)S(1)} %get-tuple-element.73.gt_ref, bf16[512,3072]{1,0:T(8,128)(2,1)S(1)} %get-tuple-element.58.refs_9_.qt_ref, f32[2048,512]{1,0:T(8,128)} %mol.6.refs_0_), custom_call_target="tpu_custom_call", output_to_operand_aliasing={{}: (2, {})} | custom-call | flops 1610612736 | bytes 7340032 | tf_op jit(solution)/shard_map/mol/pallas_call | solution.py:354
  (68 shorter events, 18.8 us)
Async XLA Ops:
  2.4 13.3 %collective-permute-start.4 = (bf16[400,512]{1,0:T(8,128)(2,1)S(1)}, bf16[400,512]{1,0:T(8,128)(2,1)S(1)}, u32[]{:S(2)}, u32[]{:S(2)}) collective-permute-start(bf16[400,512]{1,0:T(8,128)(2,1)S(1)} %pad_maximum_fusion.refs_1_), channel_id=1, source_target_pairs={{0,2},{1,3},{2,0},{3,1},{4,6},{5,7},{6,4},{7,5},{8,10},{9,11},{10,... | collective-permute-start | bytes 1228808 | tf_op jit(solution)/shard_map/ppermute | solution.py:266
  5.4 19.7 %collective-permute-start.2 = (bf16[400,512]{1,0:T(8,128)(2,1)S(1)}, bf16[400,512]{1,0:T(8,128)(2,1)S(1)}, u32[]{:S(2)}, u32[]{:S(2)}) collective-permute-start(bf16[400,512]{1,0:T(8,128)(2,1)S(1)} %pad_maximum_fusion.refs_1_), channel_id=1, source_target_pairs={{0,4},{1,5},{2,6},{3,7},{4,0},{5,1},{6,2},{7,3},{8,12},{9,13},{10,... | collective-permute-start | bytes 1228808 | tf_op jit(solution)/shard_map/ppermute | solution.py:266
  7.0 18.2 %collective-permute-start = (bf16[400,512]{1,0:T(8,128)(2,1)S(1)}, bf16[400,512]{1,0:T(8,128)(2,1)S(1)}, u32[]{:S(2)}, u32[]{:S(2)}) collective-permute-start(bf16[400,512]{1,0:T(8,128)(2,1)S(1)} %pad_maximum_fusion.refs_1_), channel_id=1, source_target_pairs={{0,6},{1,7},{2,4},{3,5},{4,2},{5,3},{6,0},{7,1},{8,14},{9,15},{10,... | collective-permute-start | bytes 1228808 | tf_op jit(solution)/shard_map/ppermute | solution.py:266
  7.0 18.7 %collective-permute-start.6 = (bf16[400,512]{1,0:T(8,128)(2,1)S(1)}, bf16[400,512]{1,0:T(8,128)(2,1)S(1)}, u32[]{:S(2)}, u32[]{:S(2)}) collective-permute-start(bf16[400,512]{1,0:T(8,128)(2,1)S(1)} %pad_maximum_fusion.refs_1_), channel_id=1, source_target_pairs={{0,1},{1,0},{2,3},{3,2},{4,5},{5,4},{6,7},{7,6},{8,9},{9,8},{10,11... | collective-permute-start | bytes 1228808 | tf_op jit(solution)/shard_map/ppermute | solution.py:266
  15.8 18.1 %collective-permute-start.5 = (bf16[400,512]{1,0:T(8,128)(2,1)S(1)}, bf16[400,512]{1,0:T(8,128)(2,1)S(1)}, u32[]{:S(2)}, u32[]{:S(2)}) collective-permute-start(bf16[400,512]{1,0:T(8,128)(2,1)S(1)} %collective-permute-done.4.refs_1_), channel_id=1, source_target_pairs={{0,1},{1,0},{2,3},{3,2},{4,5},{5,4},{6,7},{7,6},{8,9},{9,8},{10,11... | collective-permute-start | bytes 1228808 | tf_op jit(solution)/shard_map/ppermute | solution.py:266
  25.2 13.2 %collective-permute-start.3 = (bf16[400,512]{1,0:T(8,128)(2,1)S(1)}, bf16[400,512]{1,0:T(8,128)(2,1)S(1)}, u32[]{:S(2)}, u32[]{:S(2)}) collective-permute-start(bf16[400,512]{1,0:T(8,128)(2,1)S(1)} %collective-permute-done.2.refs_1_), channel_id=1, source_target_pairs={{0,1},{1,0},{2,3},{3,2},{4,5},{5,4},{6,7},{7,6},{8,9},{9,8},{10,11... | collective-permute-start | bytes 1228808 | tf_op jit(solution)/shard_map/ppermute | solution.py:266
  25.2 17.6 %collective-permute-start.1 = (bf16[400,512]{1,0:T(8,128)(2,1)S(1)}, bf16[400,512]{1,0:T(8,128)(2,1)S(1)}, u32[]{:S(2)}, u32[]{:S(2)}) collective-permute-start(bf16[400,512]{1,0:T(8,128)(2,1)S(1)} %collective-permute-done.refs_1_), channel_id=1, source_target_pairs={{0,1},{1,0},{2,3},{3,2},{4,5},{5,4},{6,7},{7,6},{8,9},{9,8},{10,11... | collective-permute-start | bytes 1228808 | tf_op jit(solution)/shard_map/ppermute | solution.py:266
  49.8 8.8 %collective-permute-start.12 = (f32[2,3072]{1,0:T(2,128)S(1)}, f32[2,3072]{1,0:T(2,128)S(1)}, u32[]{:S(2)}, u32[]{:S(2)}) collective-permute-start(f32[2,3072]{1,0:T(2,128)S(1)} %get-tuple-element.56.refs_0_), channel_id=1, source_target_pairs={{0,6},{1,7},{2,4},{3,5},{4,2},{5,3},{6,0},{7,1},{8,14},{9,15},{10,... | collective-permute-start | bytes 73736 | tf_op jit(solution)/shard_map/ppermute | solution.py:266
  51.2 7.5 %collective-permute-start.13 = (f32[2,3072]{1,0:T(2,128)S(1)}, f32[2,3072]{1,0:T(2,128)S(1)}, u32[]{:S(2)}, u32[]{:S(2)}) collective-permute-start(f32[2,3072]{1,0:T(2,128)S(1)} %get-tuple-element.56.refs_0_), channel_id=1, source_target_pairs={{0,7},{1,6},{2,5},{3,4},{4,3},{5,2},{6,1},{7,0},{8,15},{9,14},{10,... | collective-permute-start | bytes 73736 | tf_op jit(solution)/shard_map/ppermute | solution.py:266
  52.8 5.9 %collective-permute-start.7 = (f32[2,3072]{1,0:T(2,128)S(1)}, f32[2,3072]{1,0:T(2,128)S(1)}, u32[]{:S(2)}, u32[]{:S(2)}) collective-permute-start(f32[2,3072]{1,0:T(2,128)S(1)} %get-tuple-element.56.refs_0_), channel_id=1, source_target_pairs={{0,1},{1,0},{2,3},{3,2},{4,5},{5,4},{6,7},{7,6},{8,9},{9,8},{10,11... | collective-permute-start | bytes 73736 | tf_op jit(solution)/shard_map/ppermute | solution.py:266
  52.9 5.8 %collective-permute-start.8 = (f32[2,3072]{1,0:T(2,128)S(1)}, f32[2,3072]{1,0:T(2,128)S(1)}, u32[]{:S(2)}, u32[]{:S(2)}) collective-permute-start(f32[2,3072]{1,0:T(2,128)S(1)} %get-tuple-element.56.refs_0_), channel_id=1, source_target_pairs={{0,2},{1,3},{2,0},{3,1},{4,6},{5,7},{6,4},{7,5},{8,10},{9,11},{10,... | collective-permute-start | bytes 73736 | tf_op jit(solution)/shard_map/ppermute | solution.py:266
  75.5 7.6 %collective-permute-start.16 = (bf16[64,512]{1,0:T(8,128)(2,1)S(1)}, bf16[64,512]{1,0:T(8,128)(2,1)S(1)}, u32[]{:S(2)}, u32[]{:S(2)}) collective-permute-start(bf16[64,512]{1,0:T(8,128)(2,1)S(1)} %get-tuple-element.67), channel_id=1, source_target_pairs={{0,3},{1,2},{2,1},{3,0},{4,7},{5,6},{6,5},{7,4},{8,11},{9,10},{10,... | collective-permute-start | bytes 196616 | tf_op jit(solution)/shard_map/ppermute | solution.py:266
  75.9 7.2 %collective-permute-start.17 = (bf16[64,512]{1,0:T(8,128)(2,1)S(1)}, bf16[64,512]{1,0:T(8,128)(2,1)S(1)}, u32[]{:S(2)}, u32[]{:S(2)}) collective-permute-start(bf16[64,512]{1,0:T(8,128)(2,1)S(1)} %get-tuple-element.68), channel_id=1, source_target_pairs={{0,4},{1,5},{2,6},{3,7},{4,0},{5,1},{6,2},{7,3},{8,12},{9,13},{10,... | collective-permute-start | bytes 196616 | tf_op jit(solution)/shard_map/ppermute | solution.py:266
  77.4 6.3 %collective-permute-start.18 = (bf16[64,512]{1,0:T(8,128)(2,1)S(1)}, bf16[64,512]{1,0:T(8,128)(2,1)S(1)}, u32[]{:S(2)}, u32[]{:S(2)}) collective-permute-start(bf16[64,512]{1,0:T(8,128)(2,1)S(1)} %get-tuple-element.69), channel_id=1, source_target_pairs={{0,5},{1,4},{2,7},{3,6},{4,1},{5,0},{6,3},{7,2},{8,13},{9,12},{10,... | collective-permute-start | bytes 196616 | tf_op jit(solution)/shard_map/ppermute | solution.py:266
  78.0 5.8 %collective-permute-start.19 = (bf16[64,512]{1,0:T(8,128)(2,1)S(1)}, bf16[64,512]{1,0:T(8,128)(2,1)S(1)}, u32[]{:S(2)}, u32[]{:S(2)}) collective-permute-start(bf16[64,512]{1,0:T(8,128)(2,1)S(1)} %get-tuple-element.70), channel_id=1, source_target_pairs={{0,6},{1,7},{2,4},{3,5},{4,2},{5,3},{6,0},{7,1},{8,14},{9,15},{10,... | collective-permute-start | bytes 196616 | tf_op jit(solution)/shard_map/ppermute | solution.py:266
  84.6 7.3 %collective-permute-start.21 = (bf16[80,512]{1,0:T(8,128)(2,1)S(1)}, bf16[80,512]{1,0:T(8,128)(2,1)S(1)}, u32[]{:S(2)}, u32[]{:S(2)}) collective-permute-start(bf16[80,512]{1,0:T(8,128)(2,1)S(1)} %fold.1.refs_0_), channel_id=1, source_target_pairs={{0,8},{8,0},{16,24},{24,16},{1,9},{9,1},{17,25},{25,17},{2,10},{10... | collective-permute-start | bytes 245768 | tf_op jit(solution)/shard_map/ppermute | solution.py:382
  86.2 9.5 %collective-permute-start.22 = (bf16[80,512]{1,0:T(8,128)(2,1)S(1)}, bf16[80,512]{1,0:T(8,128)(2,1)S(1)}, u32[]{:S(2)}, u32[]{:S(2)}) collective-permute-start(bf16[80,512]{1,0:T(8,128)(2,1)S(1)} %fold.1.refs_0_), channel_id=1, source_target_pairs={{0,16},{8,24},{16,0},{24,8},{1,17},{9,25},{17,1},{25,9},{2,18},{10... | collective-permute-start | bytes 245768 | tf_op jit(solution)/shard_map/ppermute | solution.py:382
  88.8 6.9 %collective-permute-start.23 = (bf16[80,512]{1,0:T(8,128)(2,1)S(1)}, bf16[80,512]{1,0:T(8,128)(2,1)S(1)}, u32[]{:S(2)}, u32[]{:S(2)}) collective-permute-start(bf16[80,512]{1,0:T(8,128)(2,1)S(1)} %fold.1.refs_0_), channel_id=1, source_target_pairs={{0,24},{8,16},{16,8},{24,0},{1,25},{9,17},{17,9},{25,1},{2,26},{10... | collective-permute-start | bytes 245768 | tf_op jit(solution)/shard_map/ppermute | solution.py:382
  95.7 6.4 %collective-permute-start.24 = (bf16[64,512]{1,0:T(8,128)(2,1)S(1)}, bf16[64,512]{1,0:T(8,128)(2,1)S(1)}, u32[]{:S(2)}, u32[]{:S(2)}) collective-permute-start(bf16[64,512]{1,0:T(8,128)(2,1)S(1)} %get-tuple-element.72.refs_0_), channel_id=1, source_target_pairs={{0,1},{1,0},{2,3},{3,2},{4,5},{5,4},{6,7},{7,6},{8,9},{9,8},{10,11... | collective-permute-start | bytes 196616 | tf_op jit(solution)/shard_map/ppermute | solution.py:266
  95.8 8.0 %collective-permute-start.25 = (bf16[64,512]{1,0:T(8,128)(2,1)S(1)}, bf16[64,512]{1,0:T(8,128)(2,1)S(1)}, u32[]{:S(2)}, u32[]{:S(2)}) collective-permute-start(bf16[64,512]{1,0:T(8,128)(2,1)S(1)} %get-tuple-element.72.refs_0_), channel_id=1, source_target_pairs={{0,2},{1,3},{2,0},{3,1},{4,6},{5,7},{6,4},{7,5},{8,10},{9,11},{10,... | collective-permute-start | bytes 196616 | tf_op jit(solution)/shard_map/ppermute | solution.py:266
  100.1 8.7 %collective-permute-start.26 = (bf16[64,512]{1,0:T(8,128)(2,1)S(1)}, bf16[64,512]{1,0:T(8,128)(2,1)S(1)}, u32[]{:S(2)}, u32[]{:S(2)}) collective-permute-start(bf16[64,512]{1,0:T(8,128)(2,1)S(1)} %get-tuple-element.72.refs_0_), channel_id=1, source_target_pairs={{0,3},{1,2},{2,1},{3,0},{4,7},{5,6},{6,5},{7,4},{8,11},{9,10},{10,... | collective-permute-start | bytes 196616 | tf_op jit(solution)/shard_map/ppermute | solution.py:266
  100.5 8.4 %collective-permute-start.27 = (bf16[64,512]{1,0:T(8,128)(2,1)S(1)}, bf16[64,512]{1,0:T(8,128)(2,1)S(1)}, u32[]{:S(2)}, u32[]{:S(2)}) collective-permute-start(bf16[64,512]{1,0:T(8,128)(2,1)S(1)} %get-tuple-element.72.refs_0_), channel_id=1, source_target_pairs={{0,4},{1,5},{2,6},{3,7},{4,0},{5,1},{6,2},{7,3},{8,12},{9,13},{10,... | collective-permute-start | bytes 196616 | tf_op jit(solution)/shard_map/ppermute | solution.py:266
  101.9 7.0 %collective-permute-start.28 = (bf16[64,512]{1,0:T(8,128)(2,1)S(1)}, bf16[64,512]{1,0:T(8,128)(2,1)S(1)}, u32[]{:S(2)}, u32[]{:S(2)}) collective-permute-start(bf16[64,512]{1,0:T(8,128)(2,1)S(1)} %get-tuple-element.72.refs_0_), channel_id=1, source_target_pairs={{0,5},{1,4},{2,7},{3,6},{4,1},{5,0},{6,3},{7,2},{8,13},{9,12},{10,... | collective-permute-start | bytes 196616 | tf_op jit(solution)/shard_map/ppermute | solution.py:266
  102.2 6.7 %collective-permute-start.29 = (bf16[64,512]{1,0:T(8,128)(2,1)S(1)}, bf16[64,512]{1,0:T(8,128)(2,1)S(1)}, u32[]{:S(2)}, u32[]{:S(2)}) collective-permute-start(bf16[64,512]{1,0:T(8,128)(2,1)S(1)} %get-tuple-element.72.refs_0_), channel_id=1, source_target_pairs={{0,6},{1,7},{2,4},{3,5},{4,2},{5,3},{6,0},{7,1},{8,14},{9,15},{10,... | collective-permute-start | bytes 196616 | tf_op jit(solution)/shard_map/ppermute | solution.py:266
  (13 other events, 51.3 us)

commit v2 on v1

--- a/solution.py
+++ b/solution.py
@@ -14,9 +14,9 @@
 BASE = 256
 F32 = jnp.float32
 BF16 = jnp.bfloat16
-VMEM_BYTES = 24 * 1024 * 1024
+VMEM_BYTES = 16 * 1024 * 1024
 ROOM_BYTES = 36 * 1024 * 1024
-PIECES = 4
+PIECES = ((0, 2), (4, 4), (2, 2))
 
 
 def nt(a, b):
@@ -37,6 +37,20 @@
     for src, dst in ((bank_ref, bankt_ref), (mol_ref, molt_ref)):
         for r in range(0, src.shape[0], 256):
             dst[:, r : r + 256] = src[r : r + 256, :].T
+
+
+def load_kernel(digits_ref, spec_ref, *refs):
+    count = (len(refs) - 2) // 2
+    sems = refs[-1]
+    own_ref = refs[count]
+    moves = [pltpu.make_async_copy(spec_ref, own_ref.at[: spec_ref.shape[0]], sems.at[count])]
+    for i in range(count):
+        moves.append(pltpu.make_async_copy(refs[i], refs[count + 1 + i], sems.at[i]))
+    for move in moves:
+        move.start()
+    own_ref[spec_ref.shape[0] :, :] = digits_ref[...]
+    for move in moves:
+        move.wait()
 
 
 def score_kernel(rows, lanes, mol_tile, at_lane, aliased, *refs):
@@ -210,13 +224,13 @@
     out_ref[chunk:, :] = loss_ref[...]
 
 
-def share_kernel(*refs):
+def share_kernel(count, *refs):
     out_ref, loss_ref = refs[-2:]
     chunk = out_ref.shape[0]
     total = tree([r[...].astype(F32) for r in refs[:-2]])
     out_ref[...] = total[:chunk].astype(BF16)
     loss = total[chunk : chunk + 1] + total[chunk + 1 : chunk + 2] + total[chunk + 2 : chunk + 3]
-    loss_ref[...] = jnp.broadcast_to(loss[:, :128], loss_ref.shape)
+    loss_ref[0, 0] = jnp.max(loss) / count
 
 
 def place_kernel(mine_ref, *refs):
@@ -259,8 +273,19 @@
     low = ids % BASE
     digits = jnp.concatenate([high, low], axis=0).astype(BF16)
     digits = jnp.pad(digits, ((0, 16 - 2 * columns), (0, width - rows)))
-    own = jnp.concatenate([spectra, digits], axis=0)
-    own, me = lax.optimization_barrier((own, me))
+    digits, me = lax.optimization_barrier((digits, me))
+    fixed = (w_proj, fixed_library_matrix, mol_rows)
+    own, *fixed = pl.pallas_call(
+        load_kernel,
+        in_specs=[full] + [anywhere] * 4,
+        out_specs=[full] * 4,
+        out_shape=[sds((rows + 16, width), BF16)] + [sds(a.shape, BF16) for a in fixed],
+        scratch_shapes=[pltpu.SemaphoreType.DMA((4,))],
+        compiler_params=params(),
+        cost_estimate=cost(0, 4 << 20),
+        name="load",
+    )(digits, *[pltpu.with_memory_space_constraint(a, pltpu.HBM) for a in (spectra, *fixed)])
+    w_proj, fixed_library_matrix, mol_rows = fixed
 
     def swap(x, mask):
         return lax.ppermute(x, "lib", [(i, i ^ mask) for i in range(lib_size)])
@@ -329,7 +354,7 @@
     if not whole:
         grad_outs.append(sds((mol_count, width), F32))
     grads = pl.pallas_call(
-        functools.partial(grad_kernel, rows, 256, whole, lib_size),
+        functools.partial(grad_kernel, rows, pair, whole, lib_size),
         grid=(pairs,),
         in_specs=[smem] + [full] * lib_size + [spec_st, spec_q, spec_s, spec_acc, full],
         out_specs=[full] * len(grad_outs),
@@ -347,15 +372,17 @@
     gw_parts = grads[2 : 2 + lib_size]
 
     if whole:
-        piece = mol_count // PIECES
         grad_mol = []
-        for r in range(PIECES):
+        for first, piece in PIECES:
+            first, piece = mol_count * first // 8, mol_count * piece // 8
             grad_mol = [
                 pl.pallas_call(
-                    functools.partial(mol_kernel, r * piece),
+                    functools.partial(mol_kernel, first),
                     grid=(1,),
                     in_specs=[full, full] + [anywhere] * len(grad_mol),
-                    out_specs=pl.BlockSpec((piece, width), functools.partial(lambda r, i: (r, 0), r)),
+                    out_specs=pl.BlockSpec(
+                        (piece, width), functools.partial(lambda at, i: (at, 0), first // piece)
+                    ),
                     out_shape=pltpu.HBM((mol_count, width), F32),
                     input_output_aliases={2: 0} if grad_mol else {},
                     compiler_params=params(),
@@ -381,10 +408,10 @@
     for k in range(1, dp_size):
         terms.append(lax.ppermute(sent, "dp", [(i, i ^ k) for i in range(dp_size)]))
     shared, loss_sum = pl.pallas_call(
-        share_kernel,
+        functools.partial(share_kernel, rows * dp_size * lib_size),
         in_specs=[full] * dp_size,
-        out_specs=[full, full],
-        out_shape=[sds((chunk, width), BF16), sds((8, 128), F32)],
+        out_specs=[full, smem],
+        out_shape=[sds((chunk, width), BF16), sds((1, 1), F32)],
         compiler_params=params(8 << 20),
         cost_estimate=cost(0, 1 << 20),
         name="share",
@@ -399,7 +426,7 @@
         cost_estimate=cost(0, 2 << 20),
         name="place",
     )(me, *everyone)
-    loss = loss_sum[0, 0] / (rows * dp_size * lib_size)
+    loss = loss_sum.reshape(())
     return (grad_w, grad_mol, loss)
 
 

time: 111 us -> 108 us (0.973)
  local copies, waits for them, and re-layouts: 4.38 us -> 0 us
  waiting for transfers between devices: 23.5 us -> 27.3 us
  between operations: 2.63 us -> 0.8 us
    unnamed x12 -> x0, local copies, waits for them, and re-layouts: 3.87 us -> none
    ppermute x28, waiting for transfers between devices: 19.6 us -> 23.5 us  [swap(): return lax.ppermute(x, 'lib', [(i, i ^ mask) for i in range(lib_size)])]
  transfers between devices with their start and end apart: 31 -> 31, of which waited for: 5 -> 7; matrix products, arithmetic and copies ran while one was open for 0% -> 0% of each run, Pallas kernels for 26% -> 26%
where the time goes in v2:
time: 108 us
  Pallas kernels  50.6 us (47%)
  starting transfers between devices  28.6 us (26%)
  waiting for transfers between devices  27.3 us (25%)
    ppermute x28, starting transfers between devices, swap(): return lax.ppermute(x, 'lib', [(i, i ^ mask) for i in range(lib_size)])  24.1 us
    ppermute x28, waiting for transfers between devices, swap(): return lax.ppermute(x, 'lib', [(i, i ^ mask) for i in range(lib_size)])  23.5 us
    pallas_call x4, Pallas kernels, per_device(): pl.pallas_call(functools.partial(score_kernel, rows, 256, 1024, p * pair...  17.6 us
    pallas_call x1, Pallas kernels, per_device(): pl.pallas_call(functools.partial(grad_kernel, rows, pair, whole, lib_size...  13.7 us
    pallas_call x3, Pallas kernels, per_device(): pl.pallas_call(functools.partial(mol_kernel, first), grid=(1,), in_specs=...  10.4 us
    ppermute x3, starting transfers between devices, per_device(): terms.append(lax.ppermute(sent, 'dp', [(i, i ^ k) for i in range(dp_size)]))  4.45 us
    pallas_call x1, Pallas kernels, per_device(): pl.pallas_call(functools.partial(bank_kernel, whole, pair), grid=(pairs,)...  4.02 us
    ppermute x3, waiting for transfers between devices, per_device(): terms.append(lax.ppermute(sent, 'dp', [(i, i ^ k) for i in range(dp_size)]))  3.87 us
  transfers between devices with their start and end apart: 31, of which 7 were waited for; matrix products, arithmetic and copies ran while one was open for 0% of the time, Pallas kernels for 26%

profile of v2, /device:TPU:0, one launch (start us, length us, event | category | flops | bytes accessed | tf_op | source)
XLA Modules:
  0.0 108.1 jit_solution(8605489970272290302)
XLA Ops:
  1.4 2.2 %load.1 = (bf16[400,512]{1,0:T(8,128)(2,1)S(1)}, bf16[512,512]{1,0:T(8,128)(2,1)S(1)}, bf16[1024,512]{1,0:T(8,128)(2,1)S(1)}, bf16[2048,512]{1,0:T(8,128)(2,1)S(1)}) custom-call(bf16[16,512]{1,0:T(8,128)(2,1)S(1)} %fusion.5.digits_ref, bf16[384,512]{1,0:T(8,128)(2,1)} %spec_ref.1, bf16[512,512]{1,0:T(8,128)(2,1)} %refs_0_.1, bf16[1024,512]{1,0:T(8,128)(2,1)} %refs_1_.1, ...), custom_call_target="tpu_custom_call" | custom-call | bytes 4194304 | tf_op jit(solution)/shard_map/load/pallas_call | solution.py:278
  3.6 3.0 %collective-permute-start.4 = (bf16[400,512]{1,0:T(8,128)(2,1)S(1)}, bf16[400,512]{1,0:T(8,128)(2,1)S(1)}, u32[]{:S(2)}, u32[]{:S(2)}) collective-permute-start(bf16[400,512]{1,0:T(8,128)(2,1)S(1)} %get-tuple-element.45.refs_1_), channel_id=1, source_target_pairs={{0,2},{1,3},{2,0},{3,1},{4,6},{5,7},{6,4},{7,5},{8,10},{9,11},{10,... | collective-permute-start | bytes 1228808 | tf_op jit(solution)/shard_map/ppermute | solution.py:291
  6.7 1.5 %collective-permute-start.2 = (bf16[400,512]{1,0:T(8,128)(2,1)S(1)}, bf16[400,512]{1,0:T(8,128)(2,1)S(1)}, u32[]{:S(2)}, u32[]{:S(2)}) collective-permute-start(bf16[400,512]{1,0:T(8,128)(2,1)S(1)} %get-tuple-element.45.refs_1_), channel_id=1, source_target_pairs={{0,4},{1,5},{2,6},{3,7},{4,0},{5,1},{6,2},{7,3},{8,12},{9,13},{10,... | collective-permute-start | bytes 1228808 | tf_op jit(solution)/shard_map/ppermute | solution.py:291
  8.2 8.8 %collective-permute-done.4.refs_1_ = bf16[400,512]{1,0:T(8,128)(2,1)S(1)} collective-permute-done((bf16[400,512]{1,0:T(8,128)(2,1)S(1)}, bf16[400,512]{1,0:T(8,128)(2,1)S(1)}, u32[]{:S(2)}, u32[]{:S(2)}) %collective-permute-start.4) | collective-permute-done | bytes 409632 | tf_op jit(solution)/shard_map/ppermute | solution.py:291
  17.0 9.4 %collective-permute-done.2.refs_1_ = bf16[400,512]{1,0:T(8,128)(2,1)S(1)} collective-permute-done((bf16[400,512]{1,0:T(8,128)(2,1)S(1)}, bf16[400,512]{1,0:T(8,128)(2,1)S(1)}, u32[]{:S(2)}, u32[]{:S(2)}) %collective-permute-start.2) | collective-permute-done | bytes 409632 | tf_op jit(solution)/shard_map/ppermute | solution.py:291
  26.9 4.4 %score.4 = (bf16[512,3072]{1,0:T(8,128)(2,1)S(1)}, bf16[3072,512]{1,0:T(8,128)(2,1)S(1)}, bf16[1024,3072]{1,0:T(8,128)(2,1)S(1)}, f32[16,3072]{1,0:T(8,128)S(1)}, f32[2,3072]{1,0:T(2,128)S(1)}) custom-call(s32[1]{0:T(128)} %bitcast.1.refs_0_.mine_ref, bf16[400,512]{1,0:T(8,128)(2,1)S(1)} %get-tuple-element.45.refs_1_, ...), custom_call_target="tpu_custom_call" | custom-call | flops 2818572288 | bytes 8388608 | tf_op jit(solution)/shard_map/score/pallas_call | solution.py:311
  31.3 4.4 %score.5 = (bf16[512,3072]{1,0:T(8,128)(2,1)S(1)}, bf16[3072,512]{1,0:T(8,128)(2,1)S(1)}, bf16[1024,3072]{1,0:T(8,128)(2,1)S(1)}, f32[16,3072]{1,0:T(8,128)S(1)}, f32[2,3072]{1,0:T(2,128)S(1)}) custom-call(s32[1]{0:T(128)} %bitcast.1.refs_0_.mine_ref, ...), custom_call_target="tpu_custom_call", output_to_operand_aliasing={{0}: (6, {}), {1}: (7, {}), {2}: (8, {}), {3}: (9, {}), {4}... | custom-call | flops 2818572288 | bytes 8388608 | tf_op jit(solution)/shard_map/score/pallas_call | solution.py:311
  35.6 4.4 %score.6 = (bf16[512,3072]{1,0:T(8,128)(2,1)S(1)}, bf16[3072,512]{1,0:T(8,128)(2,1)S(1)}, bf16[1024,3072]{1,0:T(8,128)(2,1)S(1)}, f32[16,3072]{1,0:T(8,128)S(1)}, f32[2,3072]{1,0:T(2,128)S(1)}) custom-call(s32[1]{0:T(128)} %bitcast.1.refs_0_.mine_ref, ...), custom_call_target="tpu_custom_call", output_to_operand_aliasing={{0}: (6, {}), {1}: (7, {}), {2}: (8, {}), {3}: (9, {}), {4}... | custom-call | flops 2818572288 | bytes 8388608 | tf_op jit(solution)/shard_map/score/pallas_call | solution.py:311
  40.0 4.5 %score.7 = (bf16[512,3072]{1,0:T(8,128)(2,1)S(1)}, bf16[3072,512]{1,0:T(8,128)(2,1)S(1)}, bf16[1024,3072]{1,0:T(8,128)(2,1)S(1)}, f32[16,3072]{1,0:T(8,128)S(1)}, f32[2,3072]{1,0:T(2,128)S(1)}) custom-call(s32[1]{0:T(128)} %bitcast.1.refs_0_.mine_ref, ...), custom_call_target="tpu_custom_call", output_to_operand_aliasing={{0}: (6, {}), {1}: (7, {}), {2}: (8, {}), {3}: (9, {}), {4}... | custom-call | flops 2818572288 | bytes 8388608 | tf_op jit(solution)/shard_map/score/pallas_call | solution.py:311
  44.5 1.6 %collective-permute-start.10 = (f32[2,3072]{1,0:T(2,128)S(1)}, f32[2,3072]{1,0:T(2,128)S(1)}, u32[]{:S(2)}, u32[]{:S(2)}) collective-permute-start(f32[2,3072]{1,0:T(2,128)S(1)} %get-tuple-element.64.refs_0_), channel_id=1, source_target_pairs={{0,4},{1,5},{2,6},{3,7},{4,0},{5,1},{6,2},{7,3},{8,12},{9,13},{10,... | collective-permute-start | bytes 73736 | tf_op jit(solution)/shard_map/ppermute | solution.py:291
  48.4 1.5 %collective-permute-start.13 = (f32[2,3072]{1,0:T(2,128)S(1)}, f32[2,3072]{1,0:T(2,128)S(1)}, u32[]{:S(2)}, u32[]{:S(2)}) collective-permute-start(f32[2,3072]{1,0:T(2,128)S(1)} %get-tuple-element.64.refs_0_), channel_id=1, source_target_pairs={{0,7},{1,6},{2,5},{3,4},{4,3},{5,2},{6,1},{7,0},{8,15},{9,14},{10,... | collective-permute-start | bytes 73736 | tf_op jit(solution)/shard_map/ppermute | solution.py:291
  51.8 4.0 %bank.1.refs_11_ = f32[512,3072]{1,0:T(8,128)S(1)} custom-call(bf16[512,1024]{1,0:T(8,128)(2,1)S(1)} %get-tuple-element.68.bankt_ref, bf16[1024,3072]{1,0:T(8,128)(2,1)S(1)} %get-tuple-element.69.wbt_ref), custom_call_target="tpu_custom_call" | custom-call | flops 3221225472 | bytes 14680064 | tf_op jit(solution)/shard_map/bank/pallas_call | solution.py:340
  55.9 13.7 %grad.1 = (bf16[2048,3072]{1,0:T(8,128)(2,1)S(1)}, bf16[16,512]{1,0:T(8,128)(2,1)S(1)}, bf16[64,512]{1,0:T(8,128)(2,1)S(1)}, bf16[64,512]{1,0:T(8,128)(2,1)S(1)}...) custom-call(s32[1]{0:T(128)} %bitcast.1.refs_0_.mine_ref, ...), custom_call_target="tpu_custom_call" | custom-call | flops 8053063680 | bytes 25165824 | tf_op jit(solution)/shard_map/grad/pallas_call | solution.py:356
  71.5 1.5 %collective-permute-start.17 = (bf16[64,512]{1,0:T(8,128)(2,1)S(1)}, bf16[64,512]{1,0:T(8,128)(2,1)S(1)}, u32[]{:S(2)}, u32[]{:S(2)}) collective-permute-start(bf16[64,512]{1,0:T(8,128)(2,1)S(1)} %get-tuple-element.76), channel_id=1, source_target_pairs={{0,4},{1,5},{2,6},{3,7},{4,0},{5,1},{6,2},{7,3},{8,12},{9,13},{10,... | collective-permute-start | bytes 196616 | tf_op jit(solution)/shard_map/ppermute | solution.py:291
  76.5 2.9 %collective-permute-done.18.refs_5_ = bf16[64,512]{1,0:T(8,128)(2,1)S(1)} collective-permute-done((bf16[64,512]{1,0:T(8,128)(2,1)S(1)}, bf16[64,512]{1,0:T(8,128)(2,1)S(1)}, u32[]{:S(2)}, u32[]{:S(2)}) %collective-permute-start.18) | collective-permute-done | bytes 65568 | tf_op jit(solution)/shard_map/ppermute | solution.py:291
  80.2 1.6 %collective-permute-start.21 = (bf16[80,512]{1,0:T(8,128)(2,1)S(1)}, bf16[80,512]{1,0:T(8,128)(2,1)S(1)}, u32[]{:S(2)}, u32[]{:S(2)}) collective-permute-start(bf16[80,512]{1,0:T(8,128)(2,1)S(1)} %fold.1.refs_0_), channel_id=1, source_target_pairs={{0,8},{8,0},{16,24},{24,16},{1,9},{9,1},{17,25},{25,17},{2,10},{10... | collective-permute-start | bytes 245768 | tf_op jit(solution)/shard_map/ppermute | solution.py:409
  81.8 2.6 %collective-permute-start.22 = (bf16[80,512]{1,0:T(8,128)(2,1)S(1)}, bf16[80,512]{1,0:T(8,128)(2,1)S(1)}, u32[]{:S(2)}, u32[]{:S(2)}) collective-permute-start(bf16[80,512]{1,0:T(8,128)(2,1)S(1)} %fold.1.refs_0_), channel_id=1, source_target_pairs={{0,16},{8,24},{16,0},{24,8},{1,17},{9,25},{17,1},{25,9},{2,18},{10... | collective-permute-start | bytes 245768 | tf_op jit(solution)/shard_map/ppermute | solution.py:409
  84.6 2.8 %mol.3.refs_0_ = f32[2048,512]{1,0:T(8,128)} custom-call(bf16[2048,3072]{1,0:T(8,128)(2,1)S(1)} %get-tuple-element.81.gt_ref, bf16[512,3072]{1,0:T(8,128)(2,1)S(1)} %get-tuple-element.66.refs_9_.qt_ref), custom_call_target="tpu_custom_call" | custom-call | flops 1610612736 | bytes 7340032 | tf_op jit(solution)/shard_map/mol/pallas_call | solution.py:379
  87.4 3.9 %collective-permute-done.22.refs_2_ = bf16[80,512]{1,0:T(8,128)(2,1)S(1)} collective-permute-done((bf16[80,512]{1,0:T(8,128)(2,1)S(1)}, bf16[80,512]{1,0:T(8,128)(2,1)S(1)}, u32[]{:S(2)}, u32[]{:S(2)}) %collective-permute-start.22) | collective-permute-done | bytes 81952 | tf_op jit(solution)/shard_map/ppermute | solution.py:409
  92.1 1.5 %collective-permute-start.25 = (bf16[64,512]{1,0:T(8,128)(2,1)S(1)}, bf16[64,512]{1,0:T(8,128)(2,1)S(1)}, u32[]{:S(2)}, u32[]{:S(2)}) collective-permute-start(bf16[64,512]{1,0:T(8,128)(2,1)S(1)} %get-tuple-element.80.refs_0_), channel_id=1, source_target_pairs={{0,2},{1,3},{2,0},{3,1},{4,6},{5,7},{6,4},{7,5},{8,10},{9,11},{10,... | collective-permute-start | bytes 196616 | tf_op jit(solution)/shard_map/ppermute | solution.py:291
  93.6 4.8 %mol.4.refs_0_ = f32[2048,512]{1,0:T(8,128)} custom-call(bf16[2048,3072]{1,0:T(8,128)(2,1)S(1)} %get-tuple-element.81.gt_ref, bf16[512,3072]{1,0:T(8,128)(2,1)S(1)} %get-tuple-element.66.refs_9_.qt_ref, f32[2048,512]{1,0:T(8,128)} %mol.3.refs_0_), custom_call_target="tpu_custom_call", output_to_operand_aliasing={{}: (2, {})} | custom-call | flops 3221225472 | bytes 7340032 | tf_op jit(solution)/shard_map/mol/pallas_call | solution.py:379
  98.7 1.4 %collective-permute-start.27 = (bf16[64,512]{1,0:T(8,128)(2,1)S(1)}, bf16[64,512]{1,0:T(8,128)(2,1)S(1)}, u32[]{:S(2)}, u32[]{:S(2)}) collective-permute-start(bf16[64,512]{1,0:T(8,128)(2,1)S(1)} %get-tuple-element.80.refs_0_), channel_id=1, source_target_pairs={{0,4},{1,5},{2,6},{3,7},{4,0},{5,1},{6,2},{7,3},{8,12},{9,13},{10,... | collective-permute-start | bytes 196616 | tf_op jit(solution)/shard_map/ppermute | solution.py:291
  100.4 1.7 %collective-permute-start.29 = (bf16[64,512]{1,0:T(8,128)(2,1)S(1)}, bf16[64,512]{1,0:T(8,128)(2,1)S(1)}, u32[]{:S(2)}, u32[]{:S(2)}) collective-permute-start(bf16[64,512]{1,0:T(8,128)(2,1)S(1)} %get-tuple-element.80.refs_0_), channel_id=1, source_target_pairs={{0,6},{1,7},{2,4},{3,5},{4,2},{5,3},{6,0},{7,1},{8,14},{9,15},{10,... | collective-permute-start | bytes 196616 | tf_op jit(solution)/shard_map/ppermute | solution.py:291
  103.1 2.8 %mol.5 = f32[2048,512]{1,0:T(8,128)} custom-call(bf16[2048,3072]{1,0:T(8,128)(2,1)S(1)} %get-tuple-element.81.gt_ref, bf16[512,3072]{1,0:T(8,128)(2,1)S(1)} %get-tuple-element.66.refs_9_.qt_ref, f32[2048,512]{1,0:T(8,128)} %mol.4.refs_0_), custom_call_target="tpu_custom_call", output_to_operand_aliasing={{}: (2, {})} | custom-call | flops 1610612736 | bytes 7340032 | tf_op jit(solution)/shard_map/mol/pallas_call | solution.py:379
  (54 shorter events, 16.4 us)
Async XLA Ops:
  3.6 13.3 %collective-permute-start.4 = (bf16[400,512]{1,0:T(8,128)(2,1)S(1)}, bf16[400,512]{1,0:T(8,128)(2,1)S(1)}, u32[]{:S(2)}, u32[]{:S(2)}) collective-permute-start(bf16[400,512]{1,0:T(8,128)(2,1)S(1)} %get-tuple-element.45.refs_1_), channel_id=1, source_target_pairs={{0,2},{1,3},{2,0},{3,1},{4,6},{5,7},{6,4},{7,5},{8,10},{9,11},{10,... | collective-permute-start | bytes 1228808 | tf_op jit(solution)/shard_map/ppermute | solution.py:291
  6.7 19.7 %collective-permute-start.2 = (bf16[400,512]{1,0:T(8,128)(2,1)S(1)}, bf16[400,512]{1,0:T(8,128)(2,1)S(1)}, u32[]{:S(2)}, u32[]{:S(2)}) collective-permute-start(bf16[400,512]{1,0:T(8,128)(2,1)S(1)} %get-tuple-element.45.refs_1_), channel_id=1, source_target_pairs={{0,4},{1,5},{2,6},{3,7},{4,0},{5,1},{6,2},{7,3},{8,12},{9,13},{10,... | collective-permute-start | bytes 1228808 | tf_op jit(solution)/shard_map/ppermute | solution.py:291
  8.2 18.2 %collective-permute-start = (bf16[400,512]{1,0:T(8,128)(2,1)S(1)}, bf16[400,512]{1,0:T(8,128)(2,1)S(1)}, u32[]{:S(2)}, u32[]{:S(2)}) collective-permute-start(bf16[400,512]{1,0:T(8,128)(2,1)S(1)} %get-tuple-element.45.refs_1_), channel_id=1, source_target_pairs={{0,6},{1,7},{2,4},{3,5},{4,2},{5,3},{6,0},{7,1},{8,14},{9,15},{10,... | collective-permute-start | bytes 1228808 | tf_op jit(solution)/shard_map/ppermute | solution.py:291
  8.2 18.7 %collective-permute-start.6 = (bf16[400,512]{1,0:T(8,128)(2,1)S(1)}, bf16[400,512]{1,0:T(8,128)(2,1)S(1)}, u32[]{:S(2)}, u32[]{:S(2)}) collective-permute-start(bf16[400,512]{1,0:T(8,128)(2,1)S(1)} %get-tuple-element.45.refs_1_), channel_id=1, source_target_pairs={{0,1},{1,0},{2,3},{3,2},{4,5},{5,4},{6,7},{7,6},{8,9},{9,8},{10,11... | collective-permute-start | bytes 1228808 | tf_op jit(solution)/shard_map/ppermute | solution.py:291
  17.0 14.3 %collective-permute-start.5 = (bf16[400,512]{1,0:T(8,128)(2,1)S(1)}, bf16[400,512]{1,0:T(8,128)(2,1)S(1)}, u32[]{:S(2)}, u32[]{:S(2)}) collective-permute-start(bf16[400,512]{1,0:T(8,128)(2,1)S(1)} %collective-permute-done.4.refs_1_), channel_id=1, source_target_pairs={{0,1},{1,0},{2,3},{3,2},{4,5},{5,4},{6,7},{7,6},{8,9},{9,8},{10,11... | collective-permute-start | bytes 1228808 | tf_op jit(solution)/shard_map/ppermute | solution.py:291
  26.4 9.2 %collective-permute-start.3 = (bf16[400,512]{1,0:T(8,128)(2,1)S(1)}, bf16[400,512]{1,0:T(8,128)(2,1)S(1)}, u32[]{:S(2)}, u32[]{:S(2)}) collective-permute-start(bf16[400,512]{1,0:T(8,128)(2,1)S(1)} %collective-permute-done.2.refs_1_), channel_id=1, source_target_pairs={{0,1},{1,0},{2,3},{3,2},{4,5},{5,4},{6,7},{7,6},{8,9},{9,8},{10,11... | collective-permute-start | bytes 1228808 | tf_op jit(solution)/shard_map/ppermute | solution.py:291
  26.4 13.6 %collective-permute-start.1 = (bf16[400,512]{1,0:T(8,128)(2,1)S(1)}, bf16[400,512]{1,0:T(8,128)(2,1)S(1)}, u32[]{:S(2)}, u32[]{:S(2)}) collective-permute-start(bf16[400,512]{1,0:T(8,128)(2,1)S(1)} %collective-permute-done.refs_1_), channel_id=1, source_target_pairs={{0,1},{1,0},{2,3},{3,2},{4,5},{5,4},{6,7},{7,6},{8,9},{9,8},{10,11... | collective-permute-start | bytes 1228808 | tf_op jit(solution)/shard_map/ppermute | solution.py:291
  44.5 5.6 %collective-permute-start.10 = (f32[2,3072]{1,0:T(2,128)S(1)}, f32[2,3072]{1,0:T(2,128)S(1)}, u32[]{:S(2)}, u32[]{:S(2)}) collective-permute-start(f32[2,3072]{1,0:T(2,128)S(1)} %get-tuple-element.64.refs_0_), channel_id=1, source_target_pairs={{0,4},{1,5},{2,6},{3,7},{4,0},{5,1},{6,2},{7,3},{8,12},{9,13},{10,... | collective-permute-start | bytes 73736 | tf_op jit(solution)/shard_map/ppermute | solution.py:291
  47.0 8.8 %collective-permute-start.12 = (f32[2,3072]{1,0:T(2,128)S(1)}, f32[2,3072]{1,0:T(2,128)S(1)}, u32[]{:S(2)}, u32[]{:S(2)}) collective-permute-start(f32[2,3072]{1,0:T(2,128)S(1)} %get-tuple-element.64.refs_0_), channel_id=1, source_target_pairs={{0,6},{1,7},{2,4},{3,5},{4,2},{5,3},{6,0},{7,1},{8,14},{9,15},{10,... | collective-permute-start | bytes 73736 | tf_op jit(solution)/shard_map/ppermute | solution.py:291
  48.4 7.5 %collective-permute-start.13 = (f32[2,3072]{1,0:T(2,128)S(1)}, f32[2,3072]{1,0:T(2,128)S(1)}, u32[]{:S(2)}, u32[]{:S(2)}) collective-permute-start(f32[2,3072]{1,0:T(2,128)S(1)} %get-tuple-element.64.refs_0_), channel_id=1, source_target_pairs={{0,7},{1,6},{2,5},{3,4},{4,3},{5,2},{6,1},{7,0},{8,15},{9,14},{10,... | collective-permute-start | bytes 73736 | tf_op jit(solution)/shard_map/ppermute | solution.py:291
  50.0 5.9 %collective-permute-start.7 = (f32[2,3072]{1,0:T(2,128)S(1)}, f32[2,3072]{1,0:T(2,128)S(1)}, u32[]{:S(2)}, u32[]{:S(2)}) collective-permute-start(f32[2,3072]{1,0:T(2,128)S(1)} %get-tuple-element.64.refs_0_), channel_id=1, source_target_pairs={{0,1},{1,0},{2,3},{3,2},{4,5},{5,4},{6,7},{7,6},{8,9},{9,8},{10,11... | collective-permute-start | bytes 73736 | tf_op jit(solution)/shard_map/ppermute | solution.py:291
  50.2 5.8 %collective-permute-start.8 = (f32[2,3072]{1,0:T(2,128)S(1)}, f32[2,3072]{1,0:T(2,128)S(1)}, u32[]{:S(2)}, u32[]{:S(2)}) collective-permute-start(f32[2,3072]{1,0:T(2,128)S(1)} %get-tuple-element.64.refs_0_), channel_id=1, source_target_pairs={{0,2},{1,3},{2,0},{3,1},{4,6},{5,7},{6,4},{7,5},{8,10},{9,11},{10,... | collective-permute-start | bytes 73736 | tf_op jit(solution)/shard_map/ppermute | solution.py:291
  73.0 6.3 %collective-permute-start.18 = (bf16[64,512]{1,0:T(8,128)(2,1)S(1)}, bf16[64,512]{1,0:T(8,128)(2,1)S(1)}, u32[]{:S(2)}, u32[]{:S(2)}) collective-permute-start(bf16[64,512]{1,0:T(8,128)(2,1)S(1)} %get-tuple-element.77), channel_id=1, source_target_pairs={{0,5},{1,4},{2,7},{3,6},{4,1},{5,0},{6,3},{7,2},{8,13},{9,12},{10,... | collective-permute-start | bytes 196616 | tf_op jit(solution)/shard_map/ppermute | solution.py:291
  73.6 5.8 %collective-permute-start.19 = (bf16[64,512]{1,0:T(8,128)(2,1)S(1)}, bf16[64,512]{1,0:T(8,128)(2,1)S(1)}, u32[]{:S(2)}, u32[]{:S(2)}) collective-permute-start(bf16[64,512]{1,0:T(8,128)(2,1)S(1)} %get-tuple-element.78), channel_id=1, source_target_pairs={{0,6},{1,7},{2,4},{3,5},{4,2},{5,3},{6,0},{7,1},{8,14},{9,15},{10,... | collective-permute-start | bytes 196616 | tf_op jit(solution)/shard_map/ppermute | solution.py:291
  74.9 5.2 %collective-permute-start.20 = (bf16[64,512]{1,0:T(8,128)(2,1)S(1)}, bf16[64,512]{1,0:T(8,128)(2,1)S(1)}, u32[]{:S(2)}, u32[]{:S(2)}) collective-permute-start(bf16[64,512]{1,0:T(8,128)(2,1)S(1)} %get-tuple-element.79), channel_id=1, source_target_pairs={{0,7},{1,6},{2,5},{3,4},{4,3},{5,2},{6,1},{7,0},{8,15},{9,14},{10,... | collective-permute-start | bytes 196616 | tf_op jit(solution)/shard_map/ppermute | solution.py:291
  80.2 7.3 %collective-permute-start.21 = (bf16[80,512]{1,0:T(8,128)(2,1)S(1)}, bf16[80,512]{1,0:T(8,128)(2,1)S(1)}, u32[]{:S(2)}, u32[]{:S(2)}) collective-permute-start(bf16[80,512]{1,0:T(8,128)(2,1)S(1)} %fold.1.refs_0_), channel_id=1, source_target_pairs={{0,8},{8,0},{16,24},{24,16},{1,9},{9,1},{17,25},{25,17},{2,10},{10... | collective-permute-start | bytes 245768 | tf_op jit(solution)/shard_map/ppermute | solution.py:409
  81.8 9.5 %collective-permute-start.22 = (bf16[80,512]{1,0:T(8,128)(2,1)S(1)}, bf16[80,512]{1,0:T(8,128)(2,1)S(1)}, u32[]{:S(2)}, u32[]{:S(2)}) collective-permute-start(bf16[80,512]{1,0:T(8,128)(2,1)S(1)} %fold.1.refs_0_), channel_id=1, source_target_pairs={{0,16},{8,24},{16,0},{24,8},{1,17},{9,25},{17,1},{25,9},{2,18},{10... | collective-permute-start | bytes 245768 | tf_op jit(solution)/shard_map/ppermute | solution.py:409
  84.4 6.9 %collective-permute-start.23 = (bf16[80,512]{1,0:T(8,128)(2,1)S(1)}, bf16[80,512]{1,0:T(8,128)(2,1)S(1)}, u32[]{:S(2)}, u32[]{:S(2)}) collective-permute-start(bf16[80,512]{1,0:T(8,128)(2,1)S(1)} %fold.1.refs_0_), channel_id=1, source_target_pairs={{0,24},{8,16},{16,8},{24,0},{1,25},{9,17},{17,9},{25,1},{2,26},{10... | collective-permute-start | bytes 245768 | tf_op jit(solution)/shard_map/ppermute | solution.py:409
  92.0 8.4 %collective-permute-start.24 = (bf16[64,512]{1,0:T(8,128)(2,1)S(1)}, bf16[64,512]{1,0:T(8,128)(2,1)S(1)}, u32[]{:S(2)}, u32[]{:S(2)}) collective-permute-start(bf16[64,512]{1,0:T(8,128)(2,1)S(1)} %get-tuple-element.80.refs_0_), channel_id=1, source_target_pairs={{0,1},{1,0},{2,3},{3,2},{4,5},{5,4},{6,7},{7,6},{8,9},{9,8},{10,11... | collective-permute-start | bytes 196616 | tf_op jit(solution)/shard_map/ppermute | solution.py:291
  92.1 10.0 %collective-permute-start.25 = (bf16[64,512]{1,0:T(8,128)(2,1)S(1)}, bf16[64,512]{1,0:T(8,128)(2,1)S(1)}, u32[]{:S(2)}, u32[]{:S(2)}) collective-permute-start(bf16[64,512]{1,0:T(8,128)(2,1)S(1)} %get-tuple-element.80.refs_0_), channel_id=1, source_target_pairs={{0,2},{1,3},{2,0},{3,1},{4,6},{5,7},{6,4},{7,5},{8,10},{9,11},{10,... | collective-permute-start | bytes 196616 | tf_op jit(solution)/shard_map/ppermute | solution.py:291
  98.4 7.5 %collective-permute-start.26 = (bf16[64,512]{1,0:T(8,128)(2,1)S(1)}, bf16[64,512]{1,0:T(8,128)(2,1)S(1)}, u32[]{:S(2)}, u32[]{:S(2)}) collective-permute-start(bf16[64,512]{1,0:T(8,128)(2,1)S(1)} %get-tuple-element.80.refs_0_), channel_id=1, source_target_pairs={{0,3},{1,2},{2,1},{3,0},{4,7},{5,6},{6,5},{7,4},{8,11},{9,10},{10,... | collective-permute-start | bytes 196616 | tf_op jit(solution)/shard_map/ppermute | solution.py:291
  98.7 7.2 %collective-permute-start.27 = (bf16[64,512]{1,0:T(8,128)(2,1)S(1)}, bf16[64,512]{1,0:T(8,128)(2,1)S(1)}, u32[]{:S(2)}, u32[]{:S(2)}) collective-permute-start(bf16[64,512]{1,0:T(8,128)(2,1)S(1)} %get-tuple-element.80.refs_0_), channel_id=1, source_target_pairs={{0,4},{1,5},{2,6},{3,7},{4,0},{5,1},{6,2},{7,3},{8,12},{9,13},{10,... | collective-permute-start | bytes 196616 | tf_op jit(solution)/shard_map/ppermute | solution.py:291
  100.1 5.8 %collective-permute-start.28 = (bf16[64,512]{1,0:T(8,128)(2,1)S(1)}, bf16[64,512]{1,0:T(8,128)(2,1)S(1)}, u32[]{:S(2)}, u32[]{:S(2)}) collective-permute-start(bf16[64,512]{1,0:T(8,128)(2,1)S(1)} %get-tuple-element.80.refs_0_), channel_id=1, source_target_pairs={{0,5},{1,4},{2,7},{3,6},{4,1},{5,0},{6,3},{7,2},{8,13},{9,12},{10,... | collective-permute-start | bytes 196616 | tf_op jit(solution)/shard_map/ppermute | solution.py:291
  100.4 5.5 %collective-permute-start.29 = (bf16[64,512]{1,0:T(8,128)(2,1)S(1)}, bf16[64,512]{1,0:T(8,128)(2,1)S(1)}, u32[]{:S(2)}, u32[]{:S(2)}) collective-permute-start(bf16[64,512]{1,0:T(8,128)(2,1)S(1)} %get-tuple-element.80.refs_0_), channel_id=1, source_target_pairs={{0,6},{1,7},{2,4},{3,5},{4,2},{5,3},{6,0},{7,1},{8,14},{9,15},{10,... | collective-permute-start | bytes 196616 | tf_op jit(solution)/shard_map/ppermute | solution.py:291
  (7 other events, 33.3 us)

commit v3 on v2

--- a/solution.py
+++ b/solution.py
@@ -54,7 +54,7 @@
 
 
 def score_kernel(rows, lanes, mol_tile, at_lane, aliased, *refs):
-    own_ref, xa_ref, xb_ref, w_ref, bank_ref, mol_ref = refs[:6]
+    own_ref, w_ref, bank_ref, mol_ref, xa_ref, xb_ref = refs[:6]
     refs = refs[6 + aliased :]
     qt_ref, sp_ref, wbt_ref, st_ref, lse_ref, bs_ref, wt_ref = refs
     mol_count = mol_ref.shape[0]
@@ -63,8 +63,7 @@
     sp_ref[at_lane + rows : at_lane + pair, :] = xb_ref[:rows, :]
     wt_ref[...] = w_ref[...].T
     digits = jnp.concatenate(
-        [xa_ref[rows : rows + 16, :rows].astype(F32), xb_ref[rows : rows + 16, :rows].astype(F32)],
-        axis=1,
+        [x[rows : rows + 16, :rows].astype(F32) for x in (xa_ref, xb_ref)], axis=1
     )
     base = (own_ref[0] * mol_count).astype(F32)
     local = digits[0:4] * BASE + digits[4:8] - base
@@ -108,8 +107,10 @@
         )
 
 
-def bank_kernel(whole, pair, bankt_ref, wbt_ref, acc_ref):
-    cols = pl.ds(pl.multiple_of(pl.program_id(0) * pair, 256), pair) if whole else slice(None)
+def bank_kernel(whole, pair, first, bankt_ref, wbt_ref, *refs):
+    acc_ref = refs[-1]
+    at = (first + pl.program_id(0)) * pair
+    cols = pl.ds(pl.multiple_of(at, 256), pair) if whole else slice(None)
     acc_ref[:, cols] = nn(bankt_ref[...], wbt_ref[:, cols])
 
 
@@ -296,7 +297,6 @@
     blocks[1] = swap(own, 1)
     for k in range(2, lib_size, 2):
         blocks[k + 1] = swap(blocks[k], 1)
-
     outs = [
         ((width, n), BF16, (width, pair), lambda p: (0, p)),
         ((n, width), BF16, (pair, width), lambda p: (p, 0)),
@@ -304,8 +304,39 @@
         ((16, n), F32, (16, pair), lambda p: (0, p)),
         ((2, n), F32, (2, pair), lambda p: (0, p)),
     ]
-    spec_q, spec_s, spec_w, spec_st = [full if whole else pl.BlockSpec(b, f) for _, _, b, f in outs[:4]]
+    spec_q, spec_s, _, spec_st = [full if whole else pl.BlockSpec(b, f) for _, _, b, f in outs[:4]]
     spec_acc = spec_q
+
+    def turn():
+        return pl.pallas_call(
+            turn_kernel,
+            in_specs=[full] * 2,
+            out_specs=[full] * 2,
+            out_shape=[sds((a.shape[1], a.shape[0]), BF16) for a in (fixed_library_matrix, mol_rows)],
+            compiler_params=params(),
+            cost_estimate=cost(0, 8 << 20),
+            name="turn",
+        )(fixed_library_matrix, mol_rows)
+
+    def bank(first, steps, wb_t, *acc):
+        block_w, block_a = (
+            [full, full]
+            if whole
+            else [pl.BlockSpec(outs[i][2], lambda p: (0, first + p)) for i in (2, 0)]
+        )
+        return pl.pallas_call(
+            functools.partial(bank_kernel, whole, pair, first),
+            grid=(steps,),
+            in_specs=[full, block_w] + [anywhere] * len(acc),
+            out_specs=block_a,
+            out_shape=sds((width, n), F32),
+            input_output_aliases={2: 0} if acc else {},
+            compiler_params=params(),
+            cost_estimate=cost(2 * steps * pair * width * bank_count, 14 << 20),
+            name="bank",
+        )(bank_t, wb_t, *acc)
+
+    bank_t, mol_t = turn()
     state = []
     for p in range(pairs):
         state = pl.pallas_call(
@@ -322,32 +353,14 @@
             compiler_params=params(),
             cost_estimate=cost(2 * pair * width * (width + bank_count + mol_count), 8 << 20),
             name="score",
-        )(me, blocks[2 * p], blocks[2 * p + 1], w_proj, fixed_library_matrix, mol_rows, *state)
+        )(me, w_proj, fixed_library_matrix, mol_rows, blocks[2 * p], blocks[2 * p + 1], *state)
+        if p == 0:
+            acc = bank(0, 1, state[2])
     q_t, spec_all, wb_t, st, lse_own = state
 
     lse_all = [lse_own] + [swap(lse_own, m) for m in range(1, lib_size)]
 
-    bank_t, mol_t = pl.pallas_call(
-        turn_kernel,
-        in_specs=[full] * 2,
-        out_specs=[full] * 2,
-        out_shape=[sds((a.shape[1], a.shape[0]), BF16) for a in (fixed_library_matrix, mol_rows)],
-        compiler_params=params(),
-        cost_estimate=cost(0, 8 << 20),
-        name="turn",
-    )(fixed_library_matrix, mol_rows)
-
-    acc = pl.pallas_call(
-        functools.partial(bank_kernel, whole, pair),
-        grid=(pairs,),
-        in_specs=[full, spec_w],
-        out_specs=spec_acc,
-        out_shape=sds((width, n), F32),
-        compiler_params=params(),
-        cost_estimate=cost(2 * n * width * bank_count, 14 << 20),
-        name="bank",
-    )(bank_t, wb_t)
-
+    acc = bank(1, pairs - 1, wb_t, acc)
     chunk = width // lib_size
     grad_outs = [sds((mol_count, n if whole else pair), BF16), sds((16, width), BF16)]
     grad_outs += [sds((chunk, width), BF16)] * lib_size

time: 108 us -> 107 us (level)
    pallas_call x2 -> x3, Pallas kernels: 4.95 us -> 4.96 us  [the longest x2 4.03 us: bank(): pl.pallas_call(functools.partial(bank_kernel, whole, pair, first), grid=(...]
  transfers between devices with their start and end apart: 31 -> 31, of which waited for: 7 -> 7; matrix products, arithmetic and copies ran while one was open for 0% -> 0% of each run, Pallas kernels for 26% -> 27%
where the time goes in v3:
time: 107 us
  Pallas kernels  50.4 us (47%)
  starting transfers between devices  28.5 us (27%)
  waiting for transfers between devices  26.4 us (25%)
    ppermute x28, starting transfers between devices, swap(): return lax.ppermute(x, 'lib', [(i, i ^ mask) for i in range(lib_size)])  24.1 us
    ppermute x28, waiting for transfers between devices, swap(): return lax.ppermute(x, 'lib', [(i, i ^ mask) for i in range(lib_size)])  22.6 us
    pallas_call x4, Pallas kernels, per_device(): pl.pallas_call(functools.partial(score_kernel, rows, 256, 1024, p * pair...  17.4 us
    pallas_call x1, Pallas kernels, per_device(): pl.pallas_call(functools.partial(grad_kernel, rows, pair, whole, lib_size...  13.6 us
    pallas_call x3, Pallas kernels, per_device(): pl.pallas_call(functools.partial(mol_kernel, first), grid=(1,), in_specs=...  10.4 us
    ppermute x3, starting transfers between devices, per_device(): terms.append(lax.ppermute(sent, 'dp', [(i, i ^ k) for i in range(dp_size)]))  4.45 us
    pallas_call x2, Pallas kernels, bank(): pl.pallas_call(functools.partial(bank_kernel, whole, pair, first), grid=(...  4.03 us
    ppermute x3, waiting for transfers between devices, per_device(): terms.append(lax.ppermute(sent, 'dp', [(i, i ^ k) for i in range(dp_size)]))  3.81 us
  transfers between devices with their start and end apart: 31, of which 7 were waited for; matrix products, arithmetic and copies ran while one was open for 0% of the time, Pallas kernels for 27%

profile of v3, /device:TPU:0, one launch (start us, length us, event | category | flops | bytes accessed | tf_op | source)
XLA Modules:
  0.0 106.8 jit_solution(13351752976812861725)
XLA Ops:
  1.4 2.2 %load.1 = (bf16[400,512]{1,0:T(8,128)(2,1)S(1)}, bf16[512,512]{1,0:T(8,128)(2,1)S(1)}, bf16[1024,512]{1,0:T(8,128)(2,1)S(1)}, bf16[2048,512]{1,0:T(8,128)(2,1)S(1)}) custom-call(bf16[16,512]{1,0:T(8,128)(2,1)S(1)} %fusion.5.digits_ref, bf16[384,512]{1,0:T(8,128)(2,1)} %spec_ref.1, bf16[512,512]{1,0:T(8,128)(2,1)} %refs_0_.1, bf16[1024,512]{1,0:T(8,128)(2,1)} %refs_1_.1, ...), custom_call_target="tpu_custom_call" | custom-call | bytes 4194304 | tf_op jit(solution)/shard_map/load/pallas_call | solution.py:279
  3.6 3.0 %collective-permute-start.4 = (bf16[400,512]{1,0:T(8,128)(2,1)S(1)}, bf16[400,512]{1,0:T(8,128)(2,1)S(1)}, u32[]{:S(2)}, u32[]{:S(2)}) collective-permute-start(bf16[400,512]{1,0:T(8,128)(2,1)S(1)} %get-tuple-element.48.refs_4_), channel_id=1, source_target_pairs={{0,2},{1,3},{2,0},{3,1},{4,6},{5,7},{6,4},{7,5},{8,10},{9,11},{10,... | collective-permute-start | bytes 1228808 | tf_op jit(solution)/shard_map/ppermute | solution.py:292
  6.7 1.5 %collective-permute-start.2 = (bf16[400,512]{1,0:T(8,128)(2,1)S(1)}, bf16[400,512]{1,0:T(8,128)(2,1)S(1)}, u32[]{:S(2)}, u32[]{:S(2)}) collective-permute-start(bf16[400,512]{1,0:T(8,128)(2,1)S(1)} %get-tuple-element.48.refs_4_), channel_id=1, source_target_pairs={{0,4},{1,5},{2,6},{3,7},{4,0},{5,1},{6,2},{7,3},{8,12},{9,13},{10,... | collective-permute-start | bytes 1228808 | tf_op jit(solution)/shard_map/ppermute | solution.py:292
  8.2 8.8 %collective-permute-done.4.refs_4_ = bf16[400,512]{1,0:T(8,128)(2,1)S(1)} collective-permute-done((bf16[400,512]{1,0:T(8,128)(2,1)S(1)}, bf16[400,512]{1,0:T(8,128)(2,1)S(1)}, u32[]{:S(2)}, u32[]{:S(2)}) %collective-permute-start.4) | collective-permute-done | bytes 409632 | tf_op jit(solution)/shard_map/ppermute | solution.py:292
  17.9 8.4 %collective-permute-done.2.refs_4_ = bf16[400,512]{1,0:T(8,128)(2,1)S(1)} collective-permute-done((bf16[400,512]{1,0:T(8,128)(2,1)S(1)}, bf16[400,512]{1,0:T(8,128)(2,1)S(1)}, u32[]{:S(2)}, u32[]{:S(2)}) %collective-permute-start.2) | collective-permute-done | bytes 409632 | tf_op jit(solution)/shard_map/ppermute | solution.py:292
  26.9 4.3 %score.4 = (bf16[512,3072]{1,0:T(8,128)(2,1)S(1)}, bf16[3072,512]{1,0:T(8,128)(2,1)S(1)}, bf16[1024,3072]{1,0:T(8,128)(2,1)S(1)}, f32[16,3072]{1,0:T(8,128)S(1)}, f32[2,3072]{1,0:T(2,128)S(1)}) custom-call(s32[1]{0:T(128)} %bitcast.1.refs_0_.mine_ref, bf16[512,512]{1,0:T(8,128)(2,1)S(1)} %get-tuple-element.45.refs_1_, ...), custom_call_target="tpu_custom_call" | custom-call | flops 2818572288 | bytes 8388608 | tf_op jit(solution)/shard_map/score/pallas_call | solution.py:342
  32.2 4.3 %score.5 = (bf16[512,3072]{1,0:T(8,128)(2,1)S(1)}, bf16[3072,512]{1,0:T(8,128)(2,1)S(1)}, bf16[1024,3072]{1,0:T(8,128)(2,1)S(1)}, f32[16,3072]{1,0:T(8,128)S(1)}, f32[2,3072]{1,0:T(2,128)S(1)}) custom-call(s32[1]{0:T(128)} %bitcast.1.refs_0_.mine_ref, ...), custom_call_target="tpu_custom_call", output_to_operand_aliasing={{0}: (6, {}), {1}: (7, {}), {2}: (8, {}), {3}: (9, {}), {4}... | custom-call | flops 2818572288 | bytes 8388608 | tf_op jit(solution)/shard_map/score/pallas_call | solution.py:342
  36.5 4.5 %score.6 = (bf16[512,3072]{1,0:T(8,128)(2,1)S(1)}, bf16[3072,512]{1,0:T(8,128)(2,1)S(1)}, bf16[1024,3072]{1,0:T(8,128)(2,1)S(1)}, f32[16,3072]{1,0:T(8,128)S(1)}, f32[2,3072]{1,0:T(2,128)S(1)}) custom-call(s32[1]{0:T(128)} %bitcast.1.refs_0_.mine_ref, ...), custom_call_target="tpu_custom_call", output_to_operand_aliasing={{0}: (6, {}), {1}: (7, {}), {2}: (8, {}), {3}: (9, {}), {4}... | custom-call | flops 2818572288 | bytes 8388608 | tf_op jit(solution)/shard_map/score/pallas_call | solution.py:342
  41.1 4.3 %score.7 = (bf16[512,3072]{1,0:T(8,128)(2,1)S(1)}, bf16[3072,512]{1,0:T(8,128)(2,1)S(1)}, bf16[1024,3072]{1,0:T(8,128)(2,1)S(1)}, f32[16,3072]{1,0:T(8,128)S(1)}, f32[2,3072]{1,0:T(2,128)S(1)}) custom-call(s32[1]{0:T(128)} %bitcast.1.refs_0_.mine_ref, ...), custom_call_target="tpu_custom_call", output_to_operand_aliasing={{0}: (6, {}), {1}: (7, {}), {2}: (8, {}), {3}: (9, {}), {4}... | custom-call | flops 2818572288 | bytes 8388608 | tf_op jit(solution)/shard_map/score/pallas_call | solution.py:342
  45.4 1.6 %collective-permute-start.10 = (f32[2,3072]{1,0:T(2,128)S(1)}, f32[2,3072]{1,0:T(2,128)S(1)}, u32[]{:S(2)}, u32[]{:S(2)}) collective-permute-start(f32[2,3072]{1,0:T(2,128)S(1)} %get-tuple-element.64.refs_0_), channel_id=1, source_target_pairs={{0,4},{1,5},{2,6},{3,7},{4,0},{5,1},{6,2},{7,3},{8,12},{9,13},{10,... | collective-permute-start | bytes 73736 | tf_op jit(solution)/shard_map/ppermute | solution.py:292
  48.3 1.5 %collective-permute-start.13 = (f32[2,3072]{1,0:T(2,128)S(1)}, f32[2,3072]{1,0:T(2,128)S(1)}, u32[]{:S(2)}, u32[]{:S(2)}) collective-permute-start(f32[2,3072]{1,0:T(2,128)S(1)} %get-tuple-element.64.refs_0_), channel_id=1, source_target_pairs={{0,7},{1,6},{2,5},{3,4},{4,3},{5,2},{6,1},{7,0},{8,15},{9,14},{10,... | collective-permute-start | bytes 73736 | tf_op jit(solution)/shard_map/ppermute | solution.py:292
  51.7 3.0 %bank.3.refs_11_ = f32[512,3072]{1,0:T(8,128)S(1)} custom-call(bf16[512,1024]{1,0:T(8,128)(2,1)S(1)} %get-tuple-element.68.bankt_ref, bf16[1024,3072]{1,0:T(8,128)(2,1)S(1)} %get-tuple-element.69.wbt_ref, f32[512,3072]{1,0:T(8,128)S(1)} %bank.2.refs_0_), custom_call_target="tpu_custom_call", output_to_operand_aliasing={{}: (2, {})} | custom-call | flops 2415919104 | bytes 14680064 | tf_op jit(solution)/shard_map/bank/pallas_call | solution.py:327
  54.8 13.6 %grad.1 = (bf16[2048,3072]{1,0:T(8,128)(2,1)S(1)}, bf16[16,512]{1,0:T(8,128)(2,1)S(1)}, bf16[64,512]{1,0:T(8,128)(2,1)S(1)}, bf16[64,512]{1,0:T(8,128)(2,1)S(1)}...) custom-call(s32[1]{0:T(128)} %bitcast.1.refs_0_.mine_ref, ...), custom_call_target="tpu_custom_call" | custom-call | flops 8053063680 | bytes 25165824 | tf_op jit(solution)/shard_map/grad/pallas_call | solution.py:369
  70.3 1.5 %collective-permute-start.17 = (bf16[64,512]{1,0:T(8,128)(2,1)S(1)}, bf16[64,512]{1,0:T(8,128)(2,1)S(1)}, u32[]{:S(2)}, u32[]{:S(2)}) collective-permute-start(bf16[64,512]{1,0:T(8,128)(2,1)S(1)} %get-tuple-element.76), channel_id=1, source_target_pairs={{0,4},{1,5},{2,6},{3,7},{4,0},{5,1},{6,2},{7,3},{8,12},{9,13},{10,... | collective-permute-start | bytes 196616 | tf_op jit(solution)/shard_map/ppermute | solution.py:292
  75.3 2.9 %collective-permute-done.18.refs_5_ = bf16[64,512]{1,0:T(8,128)(2,1)S(1)} collective-permute-done((bf16[64,512]{1,0:T(8,128)(2,1)S(1)}, bf16[64,512]{1,0:T(8,128)(2,1)S(1)}, u32[]{:S(2)}, u32[]{:S(2)}) %collective-permute-start.18) | collective-permute-done | bytes 65568 | tf_op jit(solution)/shard_map/ppermute | solution.py:292
  79.0 1.6 %collective-permute-start.21 = (bf16[80,512]{1,0:T(8,128)(2,1)S(1)}, bf16[80,512]{1,0:T(8,128)(2,1)S(1)}, u32[]{:S(2)}, u32[]{:S(2)}) collective-permute-start(bf16[80,512]{1,0:T(8,128)(2,1)S(1)} %fold.1.refs_0_), channel_id=1, source_target_pairs={{0,8},{8,0},{16,24},{24,16},{1,9},{9,1},{17,25},{25,17},{2,10},{10... | collective-permute-start | bytes 245768 | tf_op jit(solution)/shard_map/ppermute | solution.py:422
  80.6 2.8 %collective-permute-start.22 = (bf16[80,512]{1,0:T(8,128)(2,1)S(1)}, bf16[80,512]{1,0:T(8,128)(2,1)S(1)}, u32[]{:S(2)}, u32[]{:S(2)}) collective-permute-start(bf16[80,512]{1,0:T(8,128)(2,1)S(1)} %fold.1.refs_0_), channel_id=1, source_target_pairs={{0,16},{8,24},{16,0},{24,8},{1,17},{9,25},{17,1},{25,9},{2,18},{10... | collective-permute-start | bytes 245768 | tf_op jit(solution)/shard_map/ppermute | solution.py:422
  83.4 2.8 %mol.3.refs_0_ = f32[2048,512]{1,0:T(8,128)} custom-call(bf16[2048,3072]{1,0:T(8,128)(2,1)S(1)} %get-tuple-element.81.gt_ref, bf16[512,3072]{1,0:T(8,128)(2,1)S(1)} %get-tuple-element.66.refs_9_.qt_ref), custom_call_target="tpu_custom_call" | custom-call | flops 1610612736 | bytes 7340032 | tf_op jit(solution)/shard_map/mol/pallas_call | solution.py:392
  86.2 3.8 %collective-permute-done.22.refs_2_ = bf16[80,512]{1,0:T(8,128)(2,1)S(1)} collective-permute-done((bf16[80,512]{1,0:T(8,128)(2,1)S(1)}, bf16[80,512]{1,0:T(8,128)(2,1)S(1)}, u32[]{:S(2)}, u32[]{:S(2)}) %collective-permute-start.22) | collective-permute-done | bytes 81952 | tf_op jit(solution)/shard_map/ppermute | solution.py:422
  90.8 1.6 %collective-permute-start.25 = (bf16[64,512]{1,0:T(8,128)(2,1)S(1)}, bf16[64,512]{1,0:T(8,128)(2,1)S(1)}, u32[]{:S(2)}, u32[]{:S(2)}) collective-permute-start(bf16[64,512]{1,0:T(8,128)(2,1)S(1)} %get-tuple-element.80.refs_0_), channel_id=1, source_target_pairs={{0,2},{1,3},{2,0},{3,1},{4,6},{5,7},{6,4},{7,5},{8,10},{9,11},{10,... | collective-permute-start | bytes 196616 | tf_op jit(solution)/shard_map/ppermute | solution.py:292
  92.4 4.8 %mol.4.refs_0_ = f32[2048,512]{1,0:T(8,128)} custom-call(bf16[2048,3072]{1,0:T(8,128)(2,1)S(1)} %get-tuple-element.81.gt_ref, bf16[512,3072]{1,0:T(8,128)(2,1)S(1)} %get-tuple-element.66.refs_9_.qt_ref, f32[2048,512]{1,0:T(8,128)} %mol.3.refs_0_), custom_call_target="tpu_custom_call", output_to_operand_aliasing={{}: (2, {})} | custom-call | flops 3221225472 | bytes 7340032 | tf_op jit(solution)/shard_map/mol/pallas_call | solution.py:392
  97.4 1.5 %collective-permute-start.27 = (bf16[64,512]{1,0:T(8,128)(2,1)S(1)}, bf16[64,512]{1,0:T(8,128)(2,1)S(1)}, u32[]{:S(2)}, u32[]{:S(2)}) collective-permute-start(bf16[64,512]{1,0:T(8,128)(2,1)S(1)} %get-tuple-element.80.refs_0_), channel_id=1, source_target_pairs={{0,4},{1,5},{2,6},{3,7},{4,0},{5,1},{6,2},{7,3},{8,12},{9,13},{10,... | collective-permute-start | bytes 196616 | tf_op jit(solution)/shard_map/ppermute | solution.py:292
  99.1 1.7 %collective-permute-start.29 = (bf16[64,512]{1,0:T(8,128)(2,1)S(1)}, bf16[64,512]{1,0:T(8,128)(2,1)S(1)}, u32[]{:S(2)}, u32[]{:S(2)}) collective-permute-start(bf16[64,512]{1,0:T(8,128)(2,1)S(1)} %get-tuple-element.80.refs_0_), channel_id=1, source_target_pairs={{0,6},{1,7},{2,4},{3,5},{4,2},{5,3},{6,0},{7,1},{8,14},{9,15},{10,... | collective-permute-start | bytes 196616 | tf_op jit(solution)/shard_map/ppermute | solution.py:292
  101.8 2.8 %mol.5 = f32[2048,512]{1,0:T(8,128)} custom-call(bf16[2048,3072]{1,0:T(8,128)(2,1)S(1)} %get-tuple-element.81.gt_ref, bf16[512,3072]{1,0:T(8,128)(2,1)S(1)} %get-tuple-element.66.refs_9_.qt_ref, f32[2048,512]{1,0:T(8,128)} %mol.4.refs_0_), custom_call_target="tpu_custom_call", output_to_operand_aliasing={{}: (2, {})} | custom-call | flops 1610612736 | bytes 7340032 | tf_op jit(solution)/shard_map/mol/pallas_call | solution.py:392
  (55 shorter events, 17.2 us)
Async XLA Ops:
  3.6 13.3 %collective-permute-start.4 = (bf16[400,512]{1,0:T(8,128)(2,1)S(1)}, bf16[400,512]{1,0:T(8,128)(2,1)S(1)}, u32[]{:S(2)}, u32[]{:S(2)}) collective-permute-start(bf16[400,512]{1,0:T(8,128)(2,1)S(1)} %get-tuple-element.48.refs_4_), channel_id=1, source_target_pairs={{0,2},{1,3},{2,0},{3,1},{4,6},{5,7},{6,4},{7,5},{8,10},{9,11},{10,... | collective-permute-start | bytes 1228808 | tf_op jit(solution)/shard_map/ppermute | solution.py:292
  6.7 19.7 %collective-permute-start.2 = (bf16[400,512]{1,0:T(8,128)(2,1)S(1)}, bf16[400,512]{1,0:T(8,128)(2,1)S(1)}, u32[]{:S(2)}, u32[]{:S(2)}) collective-permute-start(bf16[400,512]{1,0:T(8,128)(2,1)S(1)} %get-tuple-element.48.refs_4_), channel_id=1, source_target_pairs={{0,4},{1,5},{2,6},{3,7},{4,0},{5,1},{6,2},{7,3},{8,12},{9,13},{10,... | collective-permute-start | bytes 1228808 | tf_op jit(solution)/shard_map/ppermute | solution.py:292
  8.2 18.2 %collective-permute-start = (bf16[400,512]{1,0:T(8,128)(2,1)S(1)}, bf16[400,512]{1,0:T(8,128)(2,1)S(1)}, u32[]{:S(2)}, u32[]{:S(2)}) collective-permute-start(bf16[400,512]{1,0:T(8,128)(2,1)S(1)} %get-tuple-element.48.refs_4_), channel_id=1, source_target_pairs={{0,6},{1,7},{2,4},{3,5},{4,2},{5,3},{6,0},{7,1},{8,14},{9,15},{10,... | collective-permute-start | bytes 1228808 | tf_op jit(solution)/shard_map/ppermute | solution.py:292
  8.2 18.7 %collective-permute-start.6 = (bf16[400,512]{1,0:T(8,128)(2,1)S(1)}, bf16[400,512]{1,0:T(8,128)(2,1)S(1)}, u32[]{:S(2)}, u32[]{:S(2)}) collective-permute-start(bf16[400,512]{1,0:T(8,128)(2,1)S(1)} %get-tuple-element.48.refs_4_), channel_id=1, source_target_pairs={{0,1},{1,0},{2,3},{3,2},{4,5},{5,4},{6,7},{7,6},{8,9},{9,8},{10,11... | collective-permute-start | bytes 1228808 | tf_op jit(solution)/shard_map/ppermute | solution.py:292
  17.0 15.2 %collective-permute-start.5 = (bf16[400,512]{1,0:T(8,128)(2,1)S(1)}, bf16[400,512]{1,0:T(8,128)(2,1)S(1)}, u32[]{:S(2)}, u32[]{:S(2)}) collective-permute-start(bf16[400,512]{1,0:T(8,128)(2,1)S(1)} %collective-permute-done.4.refs_4_), channel_id=1, source_target_pairs={{0,1},{1,0},{2,3},{3,2},{4,5},{5,4},{6,7},{7,6},{8,9},{9,8},{10,11... | collective-permute-start | bytes 1228808 | tf_op jit(solution)/shard_map/ppermute | solution.py:292
  26.4 10.2 %collective-permute-start.3 = (bf16[400,512]{1,0:T(8,128)(2,1)S(1)}, bf16[400,512]{1,0:T(8,128)(2,1)S(1)}, u32[]{:S(2)}, u32[]{:S(2)}) collective-permute-start(bf16[400,512]{1,0:T(8,128)(2,1)S(1)} %collective-permute-done.2.refs_4_), channel_id=1, source_target_pairs={{0,1},{1,0},{2,3},{3,2},{4,5},{5,4},{6,7},{7,6},{8,9},{9,8},{10,11... | collective-permute-start | bytes 1228808 | tf_op jit(solution)/shard_map/ppermute | solution.py:292
  26.4 14.7 %collective-permute-start.1 = (bf16[400,512]{1,0:T(8,128)(2,1)S(1)}, bf16[400,512]{1,0:T(8,128)(2,1)S(1)}, u32[]{:S(2)}, u32[]{:S(2)}) collective-permute-start(bf16[400,512]{1,0:T(8,128)(2,1)S(1)} %collective-permute-done.refs_4_), channel_id=1, source_target_pairs={{0,1},{1,0},{2,3},{3,2},{4,5},{5,4},{6,7},{7,6},{8,9},{9,8},{10,11... | collective-permute-start | bytes 1228808 | tf_op jit(solution)/shard_map/ppermute | solution.py:292
  47.0 7.8 %collective-permute-start.12 = (f32[2,3072]{1,0:T(2,128)S(1)}, f32[2,3072]{1,0:T(2,128)S(1)}, u32[]{:S(2)}, u32[]{:S(2)}) collective-permute-start(f32[2,3072]{1,0:T(2,128)S(1)} %get-tuple-element.64.refs_0_), channel_id=1, source_target_pairs={{0,6},{1,7},{2,4},{3,5},{4,2},{5,3},{6,0},{7,1},{8,14},{9,15},{10,... | collective-permute-start | bytes 73736 | tf_op jit(solution)/shard_map/ppermute | solution.py:292
  48.3 6.4 %collective-permute-start.13 = (f32[2,3072]{1,0:T(2,128)S(1)}, f32[2,3072]{1,0:T(2,128)S(1)}, u32[]{:S(2)}, u32[]{:S(2)}) collective-permute-start(f32[2,3072]{1,0:T(2,128)S(1)} %get-tuple-element.64.refs_0_), channel_id=1, source_target_pairs={{0,7},{1,6},{2,5},{3,4},{4,3},{5,2},{6,1},{7,0},{8,15},{9,14},{10,... | collective-permute-start | bytes 73736 | tf_op jit(solution)/shard_map/ppermute | solution.py:292
  49.8 4.9 %collective-permute-start.7 = (f32[2,3072]{1,0:T(2,128)S(1)}, f32[2,3072]{1,0:T(2,128)S(1)}, u32[]{:S(2)}, u32[]{:S(2)}) collective-permute-start(f32[2,3072]{1,0:T(2,128)S(1)} %get-tuple-element.64.refs_0_), channel_id=1, source_target_pairs={{0,1},{1,0},{2,3},{3,2},{4,5},{5,4},{6,7},{7,6},{8,9},{9,8},{10,11... | collective-permute-start | bytes 73736 | tf_op jit(solution)/shard_map/ppermute | solution.py:292
  70.3 4.9 %collective-permute-start.17 = (bf16[64,512]{1,0:T(8,128)(2,1)S(1)}, bf16[64,512]{1,0:T(8,128)(2,1)S(1)}, u32[]{:S(2)}, u32[]{:S(2)}) collective-permute-start(bf16[64,512]{1,0:T(8,128)(2,1)S(1)} %get-tuple-element.76), channel_id=1, source_target_pairs={{0,4},{1,5},{2,6},{3,7},{4,0},{5,1},{6,2},{7,3},{8,12},{9,13},{10,... | collective-permute-start | bytes 196616 | tf_op jit(solution)/shard_map/ppermute | solution.py:292
  71.8 6.3 %collective-permute-start.18 = (bf16[64,512]{1,0:T(8,128)(2,1)S(1)}, bf16[64,512]{1,0:T(8,128)(2,1)S(1)}, u32[]{:S(2)}, u32[]{:S(2)}) collective-permute-start(bf16[64,512]{1,0:T(8,128)(2,1)S(1)} %get-tuple-element.77), channel_id=1, source_target_pairs={{0,5},{1,4},{2,7},{3,6},{4,1},{5,0},{6,3},{7,2},{8,13},{9,12},{10,... | collective-permute-start | bytes 196616 | tf_op jit(solution)/shard_map/ppermute | solution.py:292
  72.4 5.8 %collective-permute-start.19 = (bf16[64,512]{1,0:T(8,128)(2,1)S(1)}, bf16[64,512]{1,0:T(8,128)(2,1)S(1)}, u32[]{:S(2)}, u32[]{:S(2)}) collective-permute-start(bf16[64,512]{1,0:T(8,128)(2,1)S(1)} %get-tuple-element.78), channel_id=1, source_target_pairs={{0,6},{1,7},{2,4},{3,5},{4,2},{5,3},{6,0},{7,1},{8,14},{9,15},{10,... | collective-permute-start | bytes 196616 | tf_op jit(solution)/shard_map/ppermute | solution.py:292
  73.7 5.2 %collective-permute-start.20 = (bf16[64,512]{1,0:T(8,128)(2,1)S(1)}, bf16[64,512]{1,0:T(8,128)(2,1)S(1)}, u32[]{:S(2)}, u32[]{:S(2)}) collective-permute-start(bf16[64,512]{1,0:T(8,128)(2,1)S(1)} %get-tuple-element.79), channel_id=1, source_target_pairs={{0,7},{1,6},{2,5},{3,4},{4,3},{5,2},{6,1},{7,0},{8,15},{9,14},{10,... | collective-permute-start | bytes 196616 | tf_op jit(solution)/shard_map/ppermute | solution.py:292
  79.0 7.3 %collective-permute-start.21 = (bf16[80,512]{1,0:T(8,128)(2,1)S(1)}, bf16[80,512]{1,0:T(8,128)(2,1)S(1)}, u32[]{:S(2)}, u32[]{:S(2)}) collective-permute-start(bf16[80,512]{1,0:T(8,128)(2,1)S(1)} %fold.1.refs_0_), channel_id=1, source_target_pairs={{0,8},{8,0},{16,24},{24,16},{1,9},{9,1},{17,25},{25,17},{2,10},{10... | collective-permute-start | bytes 245768 | tf_op jit(solution)/shard_map/ppermute | solution.py:422
  80.6 9.4 %collective-permute-start.22 = (bf16[80,512]{1,0:T(8,128)(2,1)S(1)}, bf16[80,512]{1,0:T(8,128)(2,1)S(1)}, u32[]{:S(2)}, u32[]{:S(2)}) collective-permute-start(bf16[80,512]{1,0:T(8,128)(2,1)S(1)} %fold.1.refs_0_), channel_id=1, source_target_pairs={{0,16},{8,24},{16,0},{24,8},{1,17},{9,25},{17,1},{25,9},{2,18},{10... | collective-permute-start | bytes 245768 | tf_op jit(solution)/shard_map/ppermute | solution.py:422
  83.4 6.7 %collective-permute-start.23 = (bf16[80,512]{1,0:T(8,128)(2,1)S(1)}, bf16[80,512]{1,0:T(8,128)(2,1)S(1)}, u32[]{:S(2)}, u32[]{:S(2)}) collective-permute-start(bf16[80,512]{1,0:T(8,128)(2,1)S(1)} %fold.1.refs_0_), channel_id=1, source_target_pairs={{0,24},{8,16},{16,8},{24,0},{1,25},{9,17},{17,9},{25,1},{2,26},{10... | collective-permute-start | bytes 245768 | tf_op jit(solution)/shard_map/ppermute | solution.py:422
  90.7 8.4 %collective-permute-start.24 = (bf16[64,512]{1,0:T(8,128)(2,1)S(1)}, bf16[64,512]{1,0:T(8,128)(2,1)S(1)}, u32[]{:S(2)}, u32[]{:S(2)}) collective-permute-start(bf16[64,512]{1,0:T(8,128)(2,1)S(1)} %get-tuple-element.80.refs_0_), channel_id=1, source_target_pairs={{0,1},{1,0},{2,3},{3,2},{4,5},{5,4},{6,7},{7,6},{8,9},{9,8},{10,11... | collective-permute-start | bytes 196616 | tf_op jit(solution)/shard_map/ppermute | solution.py:292
  90.8 10.0 %collective-permute-start.25 = (bf16[64,512]{1,0:T(8,128)(2,1)S(1)}, bf16[64,512]{1,0:T(8,128)(2,1)S(1)}, u32[]{:S(2)}, u32[]{:S(2)}) collective-permute-start(bf16[64,512]{1,0:T(8,128)(2,1)S(1)} %get-tuple-element.80.refs_0_), channel_id=1, source_target_pairs={{0,2},{1,3},{2,0},{3,1},{4,6},{5,7},{6,4},{7,5},{8,10},{9,11},{10,... | collective-permute-start | bytes 196616 | tf_op jit(solution)/shard_map/ppermute | solution.py:292
  97.2 7.5 %collective-permute-start.26 = (bf16[64,512]{1,0:T(8,128)(2,1)S(1)}, bf16[64,512]{1,0:T(8,128)(2,1)S(1)}, u32[]{:S(2)}, u32[]{:S(2)}) collective-permute-start(bf16[64,512]{1,0:T(8,128)(2,1)S(1)} %get-tuple-element.80.refs_0_), channel_id=1, source_target_pairs={{0,3},{1,2},{2,1},{3,0},{4,7},{5,6},{6,5},{7,4},{8,11},{9,10},{10,... | collective-permute-start | bytes 196616 | tf_op jit(solution)/shard_map/ppermute | solution.py:292
  97.4 7.2 %collective-permute-start.27 = (bf16[64,512]{1,0:T(8,128)(2,1)S(1)}, bf16[64,512]{1,0:T(8,128)(2,1)S(1)}, u32[]{:S(2)}, u32[]{:S(2)}) collective-permute-start(bf16[64,512]{1,0:T(8,128)(2,1)S(1)} %get-tuple-element.80.refs_0_), channel_id=1, source_target_pairs={{0,4},{1,5},{2,6},{3,7},{4,0},{5,1},{6,2},{7,3},{8,12},{9,13},{10,... | collective-permute-start | bytes 196616 | tf_op jit(solution)/shard_map/ppermute | solution.py:292
  98.9 5.7 %collective-permute-start.28 = (bf16[64,512]{1,0:T(8,128)(2,1)S(1)}, bf16[64,512]{1,0:T(8,128)(2,1)S(1)}, u32[]{:S(2)}, u32[]{:S(2)}) collective-permute-start(bf16[64,512]{1,0:T(8,128)(2,1)S(1)} %get-tuple-element.80.refs_0_), channel_id=1, source_target_pairs={{0,5},{1,4},{2,7},{3,6},{4,1},{5,0},{6,3},{7,2},{8,13},{9,12},{10,... | collective-permute-start | bytes 196616 | tf_op jit(solution)/shard_map/ppermute | solution.py:292
  99.1 5.5 %collective-permute-start.29 = (bf16[64,512]{1,0:T(8,128)(2,1)S(1)}, bf16[64,512]{1,0:T(8,128)(2,1)S(1)}, u32[]{:S(2)}, u32[]{:S(2)}) collective-permute-start(bf16[64,512]{1,0:T(8,128)(2,1)S(1)} %get-tuple-element.80.refs_0_), channel_id=1, source_target_pairs={{0,6},{1,7},{2,4},{3,5},{4,2},{5,3},{6,0},{7,1},{8,14},{9,15},{10,... | collective-permute-start | bytes 196616 | tf_op jit(solution)/shard_map/ppermute | solution.py:292
  100.9 5.0 %collective-permute-start.30 = (bf16[64,512]{1,0:T(8,128)(2,1)S(1)}, bf16[64,512]{1,0:T(8,128)(2,1)S(1)}, u32[]{:S(2)}, u32[]{:S(2)}) collective-permute-start(bf16[64,512]{1,0:T(8,128)(2,1)S(1)} %get-tuple-element.80.refs_0_), channel_id=1, source_target_pairs={{0,7},{1,6},{2,5},{3,4},{4,3},{5,2},{6,1},{7,0},{8,15},{9,14},{10,... | collective-permute-start | bytes 196616 | tf_op jit(solution)/shard_map/ppermute | solution.py:292
  (7 other events, 30.8 us)
